TPU v7x, 32 devices: a whole 2x2x4 slice. The times are simulated.
32 devices in a mesh: expert: 8 (over z, x), shard: 4 (over y, core).
Axes of the slice: x: 2, y: 2, z: 4, core: 2. Of those that a mesh axis runs over, the one named last changes fastest.
Arguments:
- block_in: bfloat16 [1024, 768], P('expert'), may hold values from -6 to 6
- qkv_weight: bfloat16 [3, 768, 768], P(None, 'expert', 'shard'), may hold values from -0.21875 to 0.21875
- out_weight: bfloat16 [768, 768], P('expert', 'shard'), may hold values from -1.25 to 1.25
- norm1_gain: bfloat16 [768], P('expert'), may hold values from 0.099609375 to 1.8984375
- norm2_gain: bfloat16 [768], P('expert'), may hold values from 0.099609375 to 1.8984375
- router_weight: bfloat16 [768, 8], P('expert'), may hold values from -0.4375 to 0.4375
- rel_bias: float32 [32, 12], P(None, 'shard'), may hold values from -4 to 4
- expert_in: bfloat16 [8, 768, 3072], P('expert', None, 'shard'), may hold values from -0.21875 to 0.21875
- expert_out: bfloat16 [8, 3072, 768], P('expert', 'shard'), may hold values from -0.109375 to 0.109375
- routes: int32 [1024, 2], P('expert'), may hold values from 0 to 7, all different within a row; in each aligned block of 128 rows (0 to 127, 128 to 255, ...) at most 64 rows name the same one
- cotangent: bfloat16 [1024, 768], P('expert'), may hold values from -6 to 6
Outputs:
- block_out: bfloat16 [1024, 768], P('expert')
- input_grad: float32 [1024, 768], P('expert')
- qkv_grad: float32 [3, 768, 768], P(None, 'expert', 'shard')
- out_grad: float32 [768, 768], P('expert', 'shard')
- norm1_grad: float32 [768], P('expert')
- norm2_grad: float32 [768], P('expert')
- router_grad: float32 [768, 8], P('expert')
- bias_grad: float32 [32, 12], P(None, 'shard')
- expert_in_grad: float32 [8, 768, 3072], P('expert', None, 'shard')
- expert_out_grad: float32 [8, 3072, 768], P('expert', 'shard')
Inputs may be any that keep to these rules, and one draw needn't show every extreme that they name: `routes`: the two experts of a token differ. In each aligned block of 128 rows (the rows of one sequence), no expert is named by more than 64 rows, a bound that some block reaches.
All inputs are finite; a program needn't handle non-finite values.
Results may differ from a plain program's by a relative error of at most 0.012.
The roundings to bfloat16 on the way count: a program that leaves them out, or rounds other values in their place, can miss the bound.
Values may be sent and summed in bfloat16 or wider, within the bound.
A program may use at most 64 MiB of HBM per device.

v0:
```python
import math

import jax
import jax.numpy as jnp
from jax import lax
from jax.sharding import PartitionSpec as P

HEAD_DIM = 64
BUCKETS = 32
MAX_DIST = 128


EPS = 1e-06


def bucket_edges():
    exact_count = BUCKETS // 2
    edge_list = []
    for bucket_id in range(1, BUCKETS):
        if bucket_id < exact_count:
            edge_list.append(bucket_id)
        else:
            edge_list.append(
                math.ceil(
                    exact_count
                    * (MAX_DIST / exact_count)
                    ** ((bucket_id - exact_count) / (BUCKETS - exact_count))
                )
            )
    return jnp.array(edge_list, dtype=jnp.int32)


def bucket_onehot(length):
    distance = lax.broadcasted_iota(jnp.int32, (length, 1), 0)
    bucket = jnp.sum((distance >= bucket_edges()[None, :]).astype(jnp.int32), axis=1)
    return (bucket[:, None] == lax.broadcasted_iota(jnp.int32, (length, BUCKETS), 1)).astype(
        jnp.float32
    )


def toeplitz(per_distance):
    head_count, length = per_distance.shape
    widened = jnp.concatenate(
        [jnp.zeros((head_count, length - 1), per_distance.dtype), per_distance], axis=1
    )
    rows_flat = jnp.broadcast_to(widened[:, None, :], (head_count, length, 2 * length - 1)).reshape(
        head_count, -1
    )
    shifted = jnp.pad(rows_flat, ((0, 0), (0, length))).reshape(head_count, length, 2 * length)[
        :, :, :length
    ]
    return jnp.flip(shifted, axis=2)


def diagonal_sums(matrix):
    head_count, length, _ = matrix.shape
    padded = jnp.pad(jnp.flip(matrix, axis=2), ((0, 0), (0, 0), (0, length))).reshape(
        head_count, -1
    )
    skewed = padded[:, : length * (2 * length - 1)].reshape(head_count, length, 2 * length - 1)
    return jnp.sum(skewed, axis=1)[:, length - 1 :]


def gelu_parts(pre_act):
    cumulative = 0.5 * (1.0 + jax.scipy.special.erf(pre_act * (1.0 / math.sqrt(2.0))))
    density = jnp.exp(-0.5 * pre_act * pre_act) * (1.0 / math.sqrt(2.0 * math.pi))
    return (pre_act * cumulative, cumulative + pre_act * density)


def normalize(matrix):
    inverse = lax.rsqrt(jnp.mean(matrix * matrix, axis=-1, keepdims=True) + EPS)
    return (matrix * inverse, inverse)


def norm_back(upstream, normed, inverse, gain_vector):
    scaled = upstream * gain_vector
    return inverse * (scaled - normed * jnp.mean(scaled * normed, axis=-1, keepdims=True))


def send_rows(row_values, slot_target, experts, capacity):
    model_width = row_values.shape[1]
    buffer = (
        jnp.zeros((experts * capacity, model_width), row_values.dtype)
        .at[slot_target]
        .set(row_values)
        .reshape(experts, capacity, model_width)
    )
    arrived = lax.all_to_all(buffer, "expert", split_axis=0, concat_axis=0, tiled=True)
    return arrived.reshape(experts * capacity, model_width)


def join_columns(column_part):
    return lax.all_gather(column_part, "shard", axis=1, tiled=True)


def return_rows(partial_value, slot_target, experts, capacity):
    summed = lax.psum_scatter(partial_value, "shard", scatter_dimension=1, tiled=True).astype(
        jnp.bfloat16
    )
    full_rows = join_columns(summed)
    model_width = full_rows.shape[1]
    returned_slots = lax.all_to_all(
        full_rows.reshape(experts, capacity, model_width),
        "expert",
        split_axis=0,
        concat_axis=0,
        tiled=True,
    )
    return returned_slots.reshape(experts * capacity, model_width)[slot_target]


def local(
    block_in,
    qkv_weight,
    out_weight,
    norm1_gain,
    norm2_gain,
    router_weight,
    rel_bias,
    expert_in,
    expert_out,
    routes,
    cotangent,
):
    length, model_width = block_in.shape
    experts = lax.axis_size("expert")
    capacity = 4 * length // experts
    score_scale = 1.0 / math.sqrt(HEAD_DIM)
    qkv_full, out_full, gain_low_one, gain_low_two, router = (
        lax.all_gather(qkv_weight, "expert", axis=1, tiled=True),
        lax.all_gather(out_weight, "expert", axis=0, tiled=True),
        lax.all_gather(norm1_gain, "expert", axis=0, tiled=True),
        lax.all_gather(norm2_gain, "expert", axis=0, tiled=True),
        lax.all_gather(router_weight, "expert", axis=0, tiled=True),
    )
    gain_one = gain_low_one.astype(jnp.float32)
    gain_two = gain_low_two.astype(jnp.float32)
    inputs = block_in.astype(jnp.float32)
    normed_one, inverse_one = normalize(inputs)
    hidden_one = (normed_one * gain_one).astype(jnp.bfloat16)
    projected = jnp.einsum(
        "td,cdj->ctj", hidden_one, qkv_full, preferred_element_type=jnp.float32
    ).astype(jnp.bfloat16)
    local_width = projected.shape[2]
    local_heads = local_width // HEAD_DIM
    queries = projected[0].reshape(length, local_heads, HEAD_DIM)
    keys_local = projected[1].reshape(length, local_heads, HEAD_DIM)
    values_local = projected[2].reshape(length, local_heads, HEAD_DIM)
    onehot_bucket = bucket_onehot(length)
    per_distance = jnp.dot(onehot_bucket, rel_bias, precision=lax.Precision.HIGHEST).T
    bias_full = toeplitz(per_distance)
    causal = lax.broadcasted_iota(jnp.int32, (length, length), 0) >= lax.broadcasted_iota(
        jnp.int32, (length, length), 1
    )

    def scores_of():
        raw_scores = (
            jnp.einsum("ihd,jhd->hij", queries, keys_local, preferred_element_type=jnp.float32)
            * score_scale
            + bias_full
        )
        return jnp.where(causal[None], raw_scores, -jnp.inf)

    scores = scores_of()
    log_total = jnp.log(jnp.sum(jnp.exp(scores), axis=-1))
    attention_low = jnp.exp(scores - log_total[..., None]).astype(jnp.bfloat16)
    attended = (
        jnp.einsum("hij,jhd->ihd", attention_low, values_local, preferred_element_type=jnp.float32)
        .astype(jnp.bfloat16)
        .reshape(length, local_width)
    )
    attn_part = jnp.einsum("tc,mc->tm", attended, out_full, preferred_element_type=jnp.float32)
    residual_one = inputs + lax.psum(attn_part, "shard")
    normed_two, inverse_two = normalize(residual_one)
    hidden_two = (normed_two * gain_two).astype(jnp.bfloat16)
    logits = jnp.dot(hidden_two, router, preferred_element_type=jnp.float32)
    expert_ids = lax.broadcasted_iota(jnp.int32, (1, 1, router.shape[1]), 2)
    route_hot = (routes[:, :, None] == expert_ids).astype(jnp.float32)
    chosen = jnp.sum(logits[:, None, :] * route_hot, axis=-1)
    chosen_exp = jnp.exp(chosen)
    gate_value = chosen_exp / jnp.sum(chosen_exp, axis=1, keepdims=True)
    flat_routes = routes.reshape(-1)
    counts_hot = (flat_routes[:, None] == expert_ids[0]).astype(jnp.int32)
    slot_index = jnp.sum((jnp.cumsum(counts_hot, axis=0) - 1) * counts_hot, axis=1)
    slot_target = flat_routes * capacity + slot_index
    arrived = send_rows(jnp.repeat(hidden_two, 2, axis=0), slot_target, experts, capacity)
    pre_act = jnp.dot(arrived, expert_in[0], preferred_element_type=jnp.float32)
    activated, gelu_slope = gelu_parts(pre_act)
    act_low = activated.astype(jnp.bfloat16)
    expert_part = jnp.dot(act_low, expert_out[0], preferred_element_type=jnp.float32)
    returned = return_rows(expert_part, slot_target, experts, capacity).reshape(
        length, 2, model_width
    )
    mixture = jnp.sum(gate_value[:, :, None] * returned.astype(jnp.float32), axis=1)
    block_out = (residual_one + mixture).astype(jnp.bfloat16)
    upstream = cotangent.astype(jnp.float32)
    gate_grad = jnp.sum(upstream[:, None, :] * returned.astype(jnp.float32), axis=-1)
    logit_pair = gate_value * (gate_grad - jnp.sum(gate_value * gate_grad, axis=1, keepdims=True))
    logit_grad = jnp.sum(logit_pair[:, :, None] * route_hot, axis=1).astype(jnp.bfloat16)
    router_local = jnp.einsum(
        "td,te->de", hidden_two, logit_grad, preferred_element_type=jnp.float32
    )
    from_router = jnp.einsum("te,de->td", logit_grad, router, preferred_element_type=jnp.float32)
    slot_grad = (
        (gate_value[:, :, None] * upstream[:, None, :])
        .astype(jnp.bfloat16)
        .reshape(2 * length, model_width)
    )
    arrived_grad = send_rows(slot_grad, slot_target, experts, capacity)
    act_grad = jnp.einsum(
        "rd,fd->rf", arrived_grad, expert_out[0], preferred_element_type=jnp.float32
    )
    pre_grad = (act_grad * gelu_slope).astype(jnp.bfloat16)
    expert_out_local = jnp.einsum(
        "rf,rd->fd", act_low, arrived_grad, preferred_element_type=jnp.float32
    )
    expert_in_local = jnp.einsum("rd,rf->df", arrived, pre_grad, preferred_element_type=jnp.float32)
    row_part = jnp.einsum("rf,df->rd", pre_grad, expert_in[0], preferred_element_type=jnp.float32)
    row_grad = return_rows(row_part, slot_target, experts, capacity).reshape(length, 2, model_width)
    hidden_two_grad = jnp.sum(row_grad.astype(jnp.float32), axis=1) + from_router
    gain_two_grad = jnp.sum(hidden_two_grad * normed_two, axis=0)
    residual_grad = upstream + norm_back(hidden_two_grad, normed_two, inverse_two, gain_two)
    residual_low = residual_grad.astype(jnp.bfloat16)
    out_local = jnp.einsum("tm,tc->mc", residual_low, attended, preferred_element_type=jnp.float32)
    attended_grad = (
        jnp.einsum("tm,mc->tc", residual_low, out_full, preferred_element_type=jnp.float32)
        .astype(jnp.bfloat16)
        .reshape(length, local_heads, HEAD_DIM)
    )
    scores = scores_of()
    attention = jnp.exp(scores - log_total[..., None])
    attention_low = attention.astype(jnp.bfloat16)
    value_grad = jnp.einsum(
        "hij,ihd->jhd", attention_low, attended_grad, preferred_element_type=jnp.float32
    )
    prob_grad = jnp.einsum(
        "ihd,jhd->hij", attended_grad, values_local, preferred_element_type=jnp.float32
    )
    row_delta = jnp.sum(
        attended_grad.astype(jnp.float32)
        * attended.reshape(length, local_heads, HEAD_DIM).astype(jnp.float32),
        axis=-1,
    ).T
    score_grad = attention * (prob_grad - row_delta[:, :, None])
    bias_local = jnp.dot(
        onehot_bucket.T, diagonal_sums(score_grad).T, precision=lax.Precision.HIGHEST
    )
    score_low = score_grad.astype(jnp.bfloat16)
    query_grad = (
        jnp.einsum("hij,jhd->ihd", score_low, keys_local, preferred_element_type=jnp.float32)
        * score_scale
    ).astype(jnp.bfloat16)
    key_grad = (
        jnp.einsum("hij,ihd->jhd", score_low, queries, preferred_element_type=jnp.float32)
        * score_scale
    ).astype(jnp.bfloat16)
    stacked = jnp.stack([query_grad, key_grad, value_grad.astype(jnp.bfloat16)]).reshape(
        3, length, local_width
    )
    qkv_local = jnp.einsum("td,ctj->cdj", hidden_one, stacked, preferred_element_type=jnp.float32)
    hidden_one_part = jnp.einsum(
        "ctj,cdj->td", stacked, qkv_full, preferred_element_type=jnp.float32
    )
    hidden_one_grad = lax.psum(hidden_one_part, "shard")
    gain_one_grad = jnp.sum(hidden_one_grad * normed_one, axis=0)
    input_grad = residual_grad + norm_back(hidden_one_grad, normed_one, inverse_one, gain_one)
    qkv_grad, out_grad, norm1_grad, norm2_grad, router_grad = (
        lax.psum_scatter(qkv_local, "expert", scatter_dimension=1, tiled=True),
        lax.psum_scatter(out_local, "expert", scatter_dimension=0, tiled=True),
        lax.psum_scatter(gain_one_grad, "expert", scatter_dimension=0, tiled=True),
        lax.psum_scatter(gain_two_grad, "expert", scatter_dimension=0, tiled=True),
        lax.psum_scatter(router_local, "expert", scatter_dimension=0, tiled=True),
    )
    bias_grad = lax.psum(bias_local, "expert")
    return (
        block_out,
        input_grad,
        qkv_grad,
        out_grad,
        norm1_grad,
        norm2_grad,
        router_grad,
        bias_grad,
        expert_in_local[None],
        expert_out_local[None],
    )


def solution(mesh):
    placed = (
        P("expert", None),
        P(None, "expert", "shard"),
        P("expert", "shard"),
        P("expert"),
        P("expert"),
        P("expert", None),
        P(None, "shard"),
        P("expert", None, "shard"),
        P("expert", "shard", None),
        P("expert", None),
        P("expert", None),
    )
    return jax.shard_map(
        local,
        mesh=mesh,
        in_specs=placed,
        out_specs=(
            P("expert", None),
            P("expert", None),
            P(None, "expert", "shard"),
            P("expert", "shard"),
            P("expert"),
            P("expert"),
            P("expert", None),
            P(None, "shard"),
            P("expert", None, "shard"),
            P("expert", "shard", None),
        ),
        check_vma=False,
    )
```

profile of v0, /device:TPU:11, one launch (start us, length us, event | category | flops | bytes accessed | tf_op | source)
XLA Modules:
  0.0 543.2 jit_solution(12645355666873666484)
XLA Ops:
  7.3 1.3 fusion.72
  9.3 0.8 dynamic-update-slice
  10.1 0.8 dynamic-update-slice.1
  11.0 11.6 %all-reduce.8 = (bf16[768]{0:T(1024)(128)(2,1)S(1)}, bf16[768]{0:T(1024)(128)(2,1)S(1)}) all-reduce(bf16[768]{0:T(1024)(128)(2,1)S(1)} %dynamic-update-slice, bf16[768]{0:T(1024)(128)(2,1)S(1)} %dynamic-update-slice.1), channel_id=1, replica_groups=mesh['expert'=8,'shard'=4] {'expert'}, use_global_device_ids=true, to_apply=%add.3 | all-reduce | flops 1536 | bytes 6144
  22.6 1.0 fusion.32
  23.7 1.0 copy.90
  24.7 37.2 %all_gather.22 = bf16[3,768,192]{2,0,1:T(4,128)(2,1)} all-gather(bf16[3,96,192]{2,0,1:T(4,128)(2,1)S(1)} %copy.90), channel_id=1, replica_groups=mesh['expert'=8,'shard'=4] {'expert'}, dimensions={1}, use_global_device_ids=true | all-gather | bytes 995328 | tf_op jit(solution)/shard_map/all_gather | solution.py:130
  61.9 2.6 copy.91
  67.6 22.4 %all_gather.23 = bf16[768,192]{1,0:T(8,128)(2,1)S(1)} all-gather(bf16[96,192]{1,0:T(8,128)(2,1)S(1)} %copy-done.31), channel_id=1, replica_groups=mesh['expert'=8,'shard'=4] {'expert'}, dimensions={0}, use_global_device_ids=true | all-gather | bytes 331776 | tf_op jit(solution)/shard_map/all_gather | solution.py:131
  90.5 1.0 fusion.73
  93.3 47.4 %all-reduce.12.cloned.1.call-done = f32[128,768]{1,0:T(8,128)} async-done(((f32[128,768]{1,0:T(8,128)}), f32[128,768]{1,0:T(8,128)}) %all-reduce.12.cloned.1.call-update) | async-done | bytes 393232 | tf_op jit(solution)/shard_map/psum | solution.py:173
  140.8 1.1 multiply_reduce_fusion.4
  142.9 1.9 scatter_custom_fusion
  144.8 22.1 %all_to_all.20 = bf16[8,64,768]{2,1,0:T(8,128)(2,1)S(1)} all-to-all(bf16[8,64,768]{2,1,0:T(8,128)(2,1)S(1)} %bitcast.116), channel_id=1, replica_groups=mesh['expert'=8,'shard'=4] {'expert'}, dimensions={0} | all-to-all | bytes 1572864 | tf_op jit(solution)/shard_map/all_to_all | solution.py:88
  167.0 1.9 multiply_convert_fusion
  168.9 0.9 copy-done.48
  169.8 2.0 fusion.8
  172.5 21.1 %all-gather = bf16[8,96,8]{1,2,0:T(8,128)(2,1)S(1)} all-gather(bf16[1,96,8]{1,2,0:T(8,128)(2,1)S(1)} %bitcast.148), channel_id=1, replica_groups=mesh['expert'=8,'shard'=4] {'expert'}, dimensions={0}, use_global_device_ids=true | all-gather | bytes 13824 | tf_op jit(solution)/shard_map/all_gather | solution.py:134
  194.6 0.8 select_reduce_fusion.1
  197.9 2.1 scatter_custom_fusion.1
  200.0 21.4 %all_to_all.21 = bf16[8,64,768]{2,1,0:T(8,128)(2,1)S(1)} all-to-all(bf16[8,64,768]{2,1,0:T(8,128)(2,1)S(1)} %bitcast.115), channel_id=1, replica_groups=mesh['expert'=8,'shard'=4] {'expert'}, dimensions={0} | all-to-all | bytes 1572864 | tf_op jit(solution)/shard_map/all_to_all | solution.py:88
  221.4 2.7 fusion.6
  224.2 1.9 fusion.10
  226.2 1.0 convert_element_type.133
  227.2 11.8 %all_gather.26 = bf16[512,768]{0,1:T(8,128)(2,1)S(1)} all-gather(bf16[512,192]{0,1:T(8,128)(2,1)S(1)} %convert_element_type.133), channel_id=1, replica_groups=mesh['expert'=8,'shard'=4] {'shard'}, dimensions={1}, use_global_device_ids=true | all-gather | bytes 983040 | tf_op jit(solution)/shard_map/all_gather | solution.py:93
  239.0 1.2 copy.99
  240.2 5.3 all-to-all-start.1
  245.5 11.9 %reduce-scatter.12.cloned.1.call-done = f32[512,192]{0,1:T(8,128)} async-done(((f32[512,768]{0,1:T(8,128)}), f32[512,192]{0,1:T(8,128)}) %reduce-scatter.12.cloned.1.call-update) | async-done | bytes 393232 | tf_op jit(solution)/shard_map/reduce_scatter | solution.py:97
  257.4 1.0 convert_element_type.140
  258.4 8.7 %all_gather.27 = bf16[512,768]{0,1:T(8,128)(2,1)S(1)} all-gather(bf16[512,192]{0,1:T(8,128)(2,1)S(1)} %convert_element_type.140), channel_id=1, replica_groups=mesh['expert'=8,'shard'=4] {'shard'}, dimensions={1}, use_global_device_ids=true | all-gather | bytes 983040 | tf_op jit(solution)/shard_map/all_gather | solution.py:93
  267.1 1.2 copy.101
  268.3 5.5 %all-to-all-start.3 = ((bf16[8,64,768]{2,1,0:T(8,128)(2,1)}), bf16[8,64,768]{2,1,0:T(8,128)(2,1)S(1)}, u32[]{:S(2)}, u32[]{:S(2)}) async-start(bf16[8,64,768]{2,1,0:T(8,128)(2,1)} %bitcast.114), calls=%async_computation.5 | async-start | bytes 1572864 | tf_op jit(solution)/shard_map/all_to_all | solution.py:102
  273.8 1.7 convert_element_type.137
  275.5 1.3 pad_clamp_fusion
  276.8 1.8 fusion.16
  278.5 2.1 gather_fusion
  280.6 1.4 reshape.260
  282.0 3.2 multiply_reduce_fusion
  285.2 0.9 copy.103
  288.2 3.2 all-to-all-done.3
  291.4 2.1 gather_fusion.1
  293.5 1.4 reshape.261
  294.9 1.7 reduce_sum.173
  296.6 2.0 multiply_reduce_fusion.2
  298.7 1.8 multiply_add_fusion
  301.5 1.3 convolution_convert_fusion
  302.8 1.0 fusion.75
  303.9 1.1 convolution_bitcast_fusion.3
  305.2 1.3 convolution_bitcast_fusion.2
  306.5 2.8 copy.116
  309.2 4.7 reshape.310
  315.0 3.4 convolution_bitcast_fusion
  318.4 1.2 fusion.40
  319.6 3.4 convolution_bitcast_fusion.1
  324.4 40.6 %reduce-scatter.18.cloned.1.call-done = f32[96,8]{1,0:T(8,128)} async-done(((f32[768,8]{1,0:T(8,128)}), f32[96,8]{1,0:T(8,128)}) %reduce-scatter.18.cloned.1.call-update) | async-done | bytes 3088
  365.1 1.5 copy.119
  366.5 33.9 %all-reduce.14.cloned.1.call-done = f32[128,768]{1,0:T(8,128)} async-done(((f32[128,768]{1,0:T(8,128)}), f32[128,768]{1,0:T(8,128)}) %all-reduce.14.cloned.1.call-update) | async-done | bytes 393232 | tf_op jit(solution)/shard_map/psum | solution.py:264
  400.5 1.2 fusion.31
  401.7 24.4 %all-reduce.7 = (f32[768]{0:T(1024)S(1)}, f32[768]{0:T(1024)S(1)}, f32[32,3]{0,1:T(4,128)}) all-reduce(f32[768]{0:T(1024)S(1)} %get-tuple-element.64, f32[768]{0:T(1024)S(1)} %copy-done.32, f32[32,3]{0,1:T(4,128)S(1)} %fusion.43), channel_id=6, replica_groups=mesh['expert'=8,'shard'=4] {'expert'}, use_global_device_ids=true, to_apply=%region_26.27.clone | all-reduce | flops 1632 | bytes 13056
  427.3 1.9 fusion.30
  429.2 41.7 %reduce-scatter.16.cloned.1.call-done = f32[96,576]{1,0:T(8,128)} async-done(((f32[768,576]{1,0:T(8,128)}), f32[96,576]{1,0:T(8,128)}) %reduce-scatter.16.cloned.1.call-update) | async-done | bytes 221200
  471.0 1.1 reshape.311
  472.1 0.8 copy.110
  472.9 63.5 %reduce-scatter.14.cloned.1.call-done = f32[96,192]{1,0:T(8,128)} async-done(((f32[768,192]{1,0:T(8,128)}), f32[96,192]{1,0:T(8,128)}) %reduce-scatter.14.cloned.1.call-update) | async-done | bytes 73744 | tf_op jit(solution)/shard_map/reduce_scatter | solution.py:269
  (182 shorter events, 16.6 us)
Async XLA Ops:
  7.2 159.8 %copy-start = (bf16[1,768,768]{2,1,0:T(8,128)(2,1)S(1)}, bf16[1,768,768]{2,1,0:T(8,128)(2,1)}, u32[]{:S(2)}) copy-start(bf16[1,768,768]{2,1,0:T(8,128)(2,1)} %param.19) | copy-start | bytes 3538948
  7.2 133.6 %all-reduce.12.cloned.1.call-start = ((), (), s32[]{:S(2)}) async-start(), calls=%async_computation.9 | async-start | bytes 786432 | tf_op jit(solution)/shard_map/psum | solution.py:173
  23.6 40.9 %copy-start.35 = (f32[128]{0:T(128)}, f32[128]{0:T(128)S(1)}, u32[]{:S(2)}) copy-start(f32[128]{0:T(128)S(1)} %add_rsqrt_fusion.1) | copy-start | bytes 1540
  61.9 2.7 copy-start.3
  64.5 2.3 copy-start.1
  64.6 0.7 copy-start.47
  64.6 1.4 copy-start.44
  65.2 24.8 %copy-start.22 = (bf16[1,128,192]{1,2,0:T(8,128)(2,1)}, bf16[1,128,192]{1,2,0:T(8,128)(2,1)S(1)}, u32[]{:S(2)}) copy-start(bf16[1,128,192]{1,2,0:T(8,128)(2,1)S(1)} %get-tuple-element.76) | copy-start | bytes 147460
  65.2 24.8 %copy-start.24 = (bf16[1,128,192]{1,2,0:T(8,128)(2,1)}, bf16[1,128,192]{1,2,0:T(8,128)(2,1)S(1)}, u32[]{:S(2)}) copy-start(bf16[1,128,192]{1,2,0:T(8,128)(2,1)S(1)} %get-tuple-element.75) | copy-start | bytes 147460
  65.2 25.1 %copy-start.27 = (bf16[1,128,192]{1,2,0:T(8,128)(2,1)}, bf16[1,128,192]{1,2,0:T(8,128)(2,1)S(1)}, u32[]{:S(2)}) copy-start(bf16[1,128,192]{1,2,0:T(8,128)(2,1)S(1)} %get-tuple-element.77) | copy-start | bytes 147460
  65.3 0.6 copy-start.45
  66.8 0.8 copy-start.31
  67.1 24.6 %copy-start.33 = (s32[128,2]{0,1:T(2,128)S(1)}, s32[128,2]{0,1:T(2,128)}, u32[]{:S(2)}) copy-start(s32[128,2]{0,1:T(2,128)} %param.21) | copy-start | bytes 3076
  90.1 51.8 %copy-start.6 = (bf16[768,192]{1,0:T(8,128)(2,1)}, bf16[768,192]{1,0:T(8,128)(2,1)S(1)}, u32[]{:S(2)}) copy-start(bf16[768,192]{1,0:T(8,128)(2,1)S(1)} %all_gather.23) | copy-start | bytes 884740
  90.3 51.6 %copy-start.14 = (f32[3,128,128]{1,2,0:T(8,128)}, f32[3,128,128]{1,2,0:T(8,128)S(1)}, u32[]{:S(2)}) copy-start(f32[3,128,128]{1,2,0:T(8,128)S(1)} %fusion.19) | copy-start | bytes 589828
  90.5 1.1 copy-start.17
  91.6 134.5 %reduce-scatter.10.cloned.1.call-start = ((), (), s32[]{:S(2)}) async-start(), calls=%async_computation.10 | async-start | bytes 1966080 | tf_op jit(solution)/shard_map/reduce_scatter | solution.py:97
  92.1 50.8 %copy-start.29 = (f32[768]{0:T(1024)}, f32[768]{0:T(1024)S(1)}, u32[]{:S(2)}) copy-start(f32[768]{0:T(1024)S(1)} %convert_element_type.129) | copy-start | bytes 9220
  93.3 51.5 %copy-start.40 = (s32[256,1]{0,1:T(1,128)}, s32[256,1]{0,1:T(1,128)S(1)}, u32[]{:S(2)}) copy-start(s32[256,1]{0,1:T(1,128)S(1)} %compare_select_fusion) | copy-start | bytes 3076
  141.9 0.5 copy-start.38
  167.0 1.9 copy-start.10
  167.0 2.8 copy-start.42
  168.9 0.9 copy-start.48
  171.8 0.7 copy-start.41
  171.8 21.9 %copy-start.8 = (bf16[128,768]{1,0:T(8,128)(2,1)S(1)}, bf16[128,768]{1,0:T(8,128)(2,1)}, u32[]{:S(2)}) copy-start(bf16[128,768]{1,0:T(8,128)(2,1)} %param.22) | copy-start | bytes 589828
  171.8 85.6 %reduce-scatter.12.cloned.1.call-start = ((), (), s32[]{:S(2)}) async-start(), calls=%async_computation.11 | async-start | bytes 1966080 | tf_op jit(solution)/shard_map/reduce_scatter | solution.py:97
  195.3 0.5 copy-start.34
  195.9 0.6 copy-start.37
  196.6 0.6 copy-start.16
  200.0 21.4 %copy-start.43 = (bf16[1,768,768]{2,1,0:T(8,128)(2,1)S(1)}, bf16[1,768,768]{2,1,0:T(8,128)(2,1)}, u32[]{:S(2)}) copy-start(bf16[1,768,768]{2,1,0:T(8,128)(2,1)} %param.20) | copy-start | bytes 3538948
  221.4 2.7 copy-start.12
  224.2 2.0 copy-start.49
  240.2 28.1 %all-to-all-start.1 = ((bf16[8,64,768]{2,1,0:T(8,128)(2,1)}), bf16[8,64,768]{2,1,0:T(8,128)(2,1)S(1)}, u32[]{:S(2)}, u32[]{:S(2)}) async-start(bf16[8,64,768]{2,1,0:T(8,128)(2,1)} %bitcast.20), calls=%async_computation.2 | async-start | bytes 1572864 | tf_op jit(solution)/shard_map/all_to_all | solution.py:102
  268.3 23.1 %all-to-all-start.3 = ((bf16[8,64,768]{2,1,0:T(8,128)(2,1)}), bf16[8,64,768]{2,1,0:T(8,128)(2,1)S(1)}, u32[]{:S(2)}, u32[]{:S(2)}) async-start(bf16[8,64,768]{2,1,0:T(8,128)(2,1)} %bitcast.114), calls=%async_computation.5 | async-start | bytes 1572864 | tf_op jit(solution)/shard_map/all_to_all | solution.py:102
  273.8 91.3 %reduce-scatter.18.cloned.1.call-start = ((), (), s32[]{:S(2)}) async-start(), calls=%async_computation.15 | async-start | bytes 442368
  293.5 3.2 copy-start.30
  293.5 3.2 copy-start.39
  293.5 5.2 copy-start.9
  296.6 3.9 copy-start.7
  298.6 2.2 copy-start.18
  298.6 2.2 copy-start.15
  298.6 2.2 copy-start.28
  298.7 2.5 copy-start.25
  298.7 2.6 copy-start.23
  300.5 3.3 copy-start.4
  300.5 3.4 copy-start.2
  301.3 3.8 copy-start.20
  301.5 3.6 copy-start.21
  301.5 3.7 copy-start.36
  302.8 2.3 copy-start.26
  303.8 96.6 %all-reduce.14.cloned.1.call-start = ((), (), s32[]{:S(2)}) async-start(), calls=%async_computation.12 | async-start | bytes 786432 | tf_op jit(solution)/shard_map/psum | solution.py:264
  305.1 165.9 %reduce-scatter.16.cloned.1.call-start = ((), (), s32[]{:S(2)}) async-start(), calls=%async_computation.14 | async-start | bytes 2211840
  313.9 1.1 copy-start.13
  313.9 222.4 %reduce-scatter.14.cloned.1.call-start = ((), (), s32[]{:S(2)}) async-start(), calls=%async_computation.13 | async-start | bytes 884736 | tf_op jit(solution)/shard_map/reduce_scatter | solution.py:269
  315.0 3.4 copy-start.5
  315.0 3.4 copy-start.19
  318.4 1.2 copy-start.11
  323.2 1.0 copy-start.46
  323.5 78.2 %copy-start.32 = (f32[768]{0:T(1024)S(1)}, f32[768]{0:T(1024)}, u32[]{:S(2)}) copy-start(f32[768]{0:T(1024)} %get-tuple-element.60) | copy-start | bytes 9220
Sparse Core Ops, SparseCore 0:
  91.7 48.9 all-reduce.11
  171.9 29.7 reduce-scatter.9
  226.3 31.0 reduce-scatter.11
  304.0 61.0 reduce-scatter.17
  367.3 33.1 all-reduce.13
  403.8 67.1 reduce-scatter.15
  474.8 61.4 reduce-scatter.13
where the time goes:
time: 549 us; the launch traced here: 543 us
  waiting for transfers between devices  243 us (44%)
  blocking collectives  181 us (33%)
  local copies, waits for them, and re-layouts  40.9 us (7%)
  matrix products  26.6 us (5%)
  other arithmetic  24.9 us (5%)
  between operations  16.2 us (3%)
  starting transfers between devices  11.3 us (2%)
    unnamed x9, waiting for transfers between devices  82.5 us
    reduce_scatter x1, waiting for transfers between devices, local(): lax.psum_scatter(out_local, 'expert', scatter_dimension=0, tiled=True)  63.5 us
    psum x1, waiting for transfers between devices, local(): residual_one = inputs + lax.psum(attn_part, 'shard')  47.4 us
    all_to_all x2, blocking collectives, send_rows(): lax.all_to_all(buffer, 'expert', split_axis=0, concat_axis=0, tiled=True)  43.5 us
    all_gather x1, blocking collectives, local(): lax.all_gather(qkv_weight, 'expert', axis=1, tiled=True)  37.2 us
    unnamed x2, blocking collectives  36 us
    psum x1, waiting for transfers between devices, local(): hidden_one_grad = lax.psum(hidden_one_part, 'shard')  33.9 us
    all_gather x1, blocking collectives, local(): lax.all_gather(out_weight, 'expert', axis=0, tiled=True)  22.4 us
  transfers between devices with their start and end apart: 9, of which 7 were waited for; matrix products, arithmetic and copies ran while one was open for 10% of the time, Pallas kernels for 0%

commit v1 on v0

--- a/solution.py
+++ b/solution.py
@@ -3,6 +3,8 @@
 import jax
 import jax.numpy as jnp
 from jax import lax
+from jax.experimental import pallas as pl
+from jax.experimental.pallas import tpu as pltpu
 from jax.sharding import PartitionSpec as P
 
 HEAD_DIM = 64
@@ -77,36 +79,234 @@
     return inverse * (scaled - normed * jnp.mean(scaled * normed, axis=-1, keepdims=True))
 
 
-def send_rows(row_values, slot_target, experts, capacity):
-    model_width = row_values.shape[1]
-    buffer = (
-        jnp.zeros((experts * capacity, model_width), row_values.dtype)
-        .at[slot_target]
-        .set(row_values)
-        .reshape(experts, capacity, model_width)
-    )
-    arrived = lax.all_to_all(buffer, "expert", split_axis=0, concat_axis=0, tiled=True)
-    return arrived.reshape(experts * capacity, model_width)
-
-
-def join_columns(column_part):
-    return lax.all_gather(column_part, "shard", axis=1, tiled=True)
-
-
-def return_rows(partial_value, slot_target, experts, capacity):
-    summed = lax.psum_scatter(partial_value, "shard", scatter_dimension=1, tiled=True).astype(
-        jnp.bfloat16
-    )
-    full_rows = join_columns(summed)
-    model_width = full_rows.shape[1]
-    returned_slots = lax.all_to_all(
-        full_rows.reshape(experts, capacity, model_width),
-        "expert",
-        split_axis=0,
-        concat_axis=0,
-        tiled=True,
-    )
-    return returned_slots.reshape(experts * capacity, model_width)[slot_target]
+MESH = pl.DeviceIdType.MESH
+DMA = pltpu.SemaphoreType.DMA
+
+
+def remote(source, target, sent, arrived, axis, peer):
+    return pltpu.make_async_remote_copy(
+        src_ref=source,
+        dst_ref=target,
+        send_sem=sent,
+        recv_sem=arrived,
+        device_id={axis: peer},
+        device_id_type=MESH,
+    )
+
+
+def greet(axis_peers):
+    barrier = pltpu.get_barrier_semaphore()
+    for axis, peer in axis_peers:
+        pl.semaphore_signal(barrier, inc=1, device_id={axis: peer}, device_id_type=MESH)
+    pl.semaphore_wait(barrier, len(axis_peers))
+
+
+def call(kernel, out_shape, scratch, collective, operands):
+    vmem = pl.BlockSpec(memory_space=pltpu.VMEM)
+    return pl.pallas_call(
+        kernel,
+        out_shape=out_shape,
+        in_specs=[vmem] * len(operands),
+        out_specs=jax.tree.map(lambda _: vmem, out_shape),
+        scratch_shapes=scratch,
+        compiler_params=pltpu.CompilerParams(collective_id=collective, has_side_effects=True),
+    )(*operands)
+
+
+def exchange(axis, collective, spread, shared):
+    count = lax.axis_size(axis)
+    operands = tuple(spread) + tuple(shared)
+    total = len(operands)
+
+    def kernel(*refs):
+        ins, outs = refs[:total], refs[total : 2 * total]
+        sent, arrived, own_sem = refs[2 * total :]
+        me = lax.axis_index(axis)
+        greet([(axis, lax.rem(me + step, count)) for step in range(1, count)])
+        copies = []
+        for step in range(1, count):
+            peer = lax.rem(me + step, count)
+            for index in range(total):
+                source = ins[index].at[peer] if index < len(spread) else ins[index]
+                copy = remote(
+                    source,
+                    outs[index].at[me],
+                    sent.at[index, step],
+                    arrived.at[index, step],
+                    axis,
+                    peer,
+                )
+                copy.start()
+                copies.append(copy)
+        for index in range(total):
+            source = ins[index].at[me] if index < len(spread) else ins[index]
+            copy = pltpu.make_async_copy(source, outs[index].at[me], own_sem.at[index])
+            copy.start()
+            copies.append(copy)
+        for copy in copies:
+            copy.wait()
+
+    out_shape = [jax.ShapeDtypeStruct(x.shape, x.dtype) for x in spread] + [
+        jax.ShapeDtypeStruct((count,) + x.shape, x.dtype) for x in shared
+    ]
+    scratch = [DMA((total, count)), DMA((total, count)), DMA((total,))]
+    return call(kernel, out_shape, scratch, collective, operands)
+
+
+def square(shard):
+    beside = shard + 1 - 2 * lax.rem(shard, 2)
+    across = lax.rem(shard + 2, 4)
+    return beside, across, lax.rem(beside + 2, 4)
+
+
+def dispatch(buffer, collective):
+    experts, capacity, width = buffer.shape
+
+    def kernel(in_ref, out_ref, sent, arrived, own_sem):
+        me, shard = lax.axis_index("expert"), lax.axis_index("shard")
+        beside, across, _ = square(shard)
+        greet(
+            [("expert", lax.rem(me + step, experts)) for step in range(1, experts)]
+            + [("shard", beside), ("shard", across)]
+        )
+        first = []
+        for step in range(1, experts):
+            peer = lax.rem(me + step, experts)
+            copy = remote(
+                in_ref.at[peer],
+                out_ref.at[shard, me],
+                sent.at[0, step],
+                arrived.at[0, step],
+                "expert",
+                peer,
+            )
+            copy.start()
+            first.append(copy)
+        own = pltpu.make_async_copy(in_ref.at[me], out_ref.at[shard, me], own_sem)
+        own.start()
+        near, far, last = [], [], []
+        for step in range(experts):
+            origin = lax.rem(me + experts - step, experts)
+            if step:
+                first[step - 1].wait_recv()
+            else:
+                own.wait()
+            block = out_ref.at[shard, origin]
+            copy = remote(block, block, sent.at[2, step], arrived.at[2, step], "shard", across)
+            copy.start()
+            far.append(copy)
+            copy = remote(block, block, sent.at[1, step], arrived.at[1, step], "shard", beside)
+            copy.start()
+            near.append(copy)
+        for step in range(experts):
+            origin = lax.rem(me + experts - step, experts)
+            far[step].wait_recv()
+            block = out_ref.at[across, origin]
+            copy = remote(block, block, sent.at[3, step], arrived.at[3, step], "shard", beside)
+            copy.start()
+            last.append(copy)
+        for copy in first + far:
+            copy.wait_send()
+        for copy in near + last:
+            copy.wait()
+
+    return call(
+        kernel,
+        jax.ShapeDtypeStruct((4, experts, capacity, width), buffer.dtype),
+        [DMA((4, experts)), DMA((4, experts)), DMA],
+        collective,
+        (buffer,),
+    )
+
+
+def give_back(parts, collective):
+    _, experts, capacity, width = parts.shape
+    block_shape = (experts, capacity, width)
+
+    def kernel(in_ref, out_ref, pair, own_sum, send_sum, far_sum, ready, sent, arrived, own_sem):
+        me, shard = lax.axis_index("expert"), lax.axis_index("shard")
+        beside, across, corner = square(shard)
+        greet(
+            [("expert", lax.rem(me + step, experts)) for step in range(1, experts)]
+            + [("shard", beside), ("shard", across)]
+        )
+        near, far, last = [], [], []
+        for step in range(experts):
+            peer = lax.rem(me + step + 1, experts)
+            for which, quarter in ((0, corner), (1, beside)):
+                copy = remote(
+                    in_ref.at[quarter, peer],
+                    pair.at[which, step],
+                    sent.at[which, step],
+                    arrived.at[which, step],
+                    "shard",
+                    beside,
+                )
+                copy.start()
+                near.append(copy)
+        for step in range(experts):
+            peer = lax.rem(me + step + 1, experts)
+            near[2 * step].wait_recv()
+            send_sum[step] = (
+                in_ref[across, peer].astype(jnp.float32) + pair[0, step].astype(jnp.float32)
+            ).astype(jnp.bfloat16)
+            copy = remote(
+                send_sum.at[step],
+                far_sum.at[step],
+                sent.at[2, step],
+                arrived.at[2, step],
+                "shard",
+                across,
+            )
+            copy.start()
+            far.append(copy)
+            near[2 * step + 1].wait_recv()
+            own_sum[step] = in_ref[shard, peer].astype(jnp.float32) + pair[1, step].astype(
+                jnp.float32
+            )
+        for step in range(experts):
+            peer = lax.rem(me + step + 1, experts)
+            far[step].wait_recv()
+            ready[step] = (own_sum[step] + far_sum[step].astype(jnp.float32)).astype(jnp.bfloat16)
+            if step < experts - 1:
+                copy = remote(
+                    ready.at[step],
+                    out_ref.at[me],
+                    sent.at[3, step],
+                    arrived.at[3, step],
+                    "expert",
+                    peer,
+                )
+            else:
+                copy = pltpu.make_async_copy(ready.at[step], out_ref.at[me], own_sem)
+            copy.start()
+            last.append(copy)
+        for copy in near + far:
+            copy.wait_send()
+        for copy in last:
+            copy.wait()
+
+    return call(
+        kernel,
+        jax.ShapeDtypeStruct(block_shape, jnp.bfloat16),
+        [
+            pltpu.VMEM((2,) + block_shape, jnp.bfloat16),
+            pltpu.VMEM(block_shape, jnp.float32),
+            pltpu.VMEM(block_shape, jnp.bfloat16),
+            pltpu.VMEM(block_shape, jnp.bfloat16),
+            pltpu.VMEM(block_shape, jnp.bfloat16),
+            DMA((4, experts)),
+            DMA((4, experts)),
+            DMA,
+        ],
+        collective,
+        (parts,),
+    )
+
+
+def sum_shards(part, collective):
+    (gathered,) = exchange("shard", collective, (), (part.astype(jnp.bfloat16),))
+    return jnp.sum(gathered.astype(jnp.float32), axis=0)
 
 
 def local(
@@ -126,13 +326,16 @@
     experts = lax.axis_size("expert")
     capacity = 4 * length // experts
     score_scale = 1.0 / math.sqrt(HEAD_DIM)
-    qkv_full, out_full, gain_low_one, gain_low_two, router = (
-        lax.all_gather(qkv_weight, "expert", axis=1, tiled=True),
-        lax.all_gather(out_weight, "expert", axis=0, tiled=True),
-        lax.all_gather(norm1_gain, "expert", axis=0, tiled=True),
-        lax.all_gather(norm2_gain, "expert", axis=0, tiled=True),
-        lax.all_gather(router_weight, "expert", axis=0, tiled=True),
-    )
+    shards = lax.axis_size("shard")
+    shard = lax.axis_index("shard")
+    quarter = model_width // shards
+    small = jnp.concatenate([norm1_gain[None], norm2_gain[None], router_weight.T], axis=0)
+    weights = jnp.concatenate([qkv_weight, out_weight[None]], axis=0)
+    weights_all, small_all = exchange("expert", 0, (), (weights, small))
+    weights_all = weights_all.transpose(1, 0, 2, 3).reshape(4, model_width, -1)
+    small_all = small_all.transpose(1, 0, 2).reshape(-1, model_width)
+    qkv_full, out_full = weights_all[:3], weights_all[3]
+    gain_low_one, gain_low_two, router = small_all[0], small_all[1], small_all[2:].T
     gain_one = gain_low_one.astype(jnp.float32)
     gain_two = gain_low_two.astype(jnp.float32)
     inputs = block_in.astype(jnp.float32)
@@ -170,7 +373,7 @@
         .reshape(length, local_width)
     )
     attn_part = jnp.einsum("tc,mc->tm", attended, out_full, preferred_element_type=jnp.float32)
-    residual_one = inputs + lax.psum(attn_part, "shard")
+    residual_one = inputs + sum_shards(attn_part, 1)
     normed_two, inverse_two = normalize(residual_one)
     hidden_two = (normed_two * gain_two).astype(jnp.bfloat16)
     logits = jnp.dot(hidden_two, router, preferred_element_type=jnp.float32)
@@ -183,41 +386,79 @@
     counts_hot = (flat_routes[:, None] == expert_ids[0]).astype(jnp.int32)
     slot_index = jnp.sum((jnp.cumsum(counts_hot, axis=0) - 1) * counts_hot, axis=1)
     slot_target = flat_routes * capacity + slot_index
-    arrived = send_rows(jnp.repeat(hidden_two, 2, axis=0), slot_target, experts, capacity)
+    upstream = cotangent.astype(jnp.float32)
+
+    def my_columns(matrix):
+        return lax.dynamic_slice_in_dim(matrix, shard * quarter, quarter, axis=1)
+
+    slots = experts * capacity
+    place = (
+        lax.broadcasted_iota(jnp.int32, (slots, 2 * length), 0) == slot_target[None, :]
+    ).astype(jnp.bfloat16)
+    hidden_rows = jnp.repeat(my_columns(hidden_two), 2, axis=0)
+    slot_grad = (
+        (gate_value[:, :, None] * my_columns(upstream)[:, None, :])
+        .astype(jnp.bfloat16)
+        .reshape(2 * length, quarter)
+    )
+    outgoing = jnp.dot(
+        place,
+        jnp.concatenate([hidden_rows, slot_grad], axis=1),
+        preferred_element_type=jnp.float32,
+    ).astype(jnp.bfloat16)
+    incoming = dispatch(outgoing.reshape(experts, capacity, 2 * quarter), 2).reshape(
+        shards, slots, 2, quarter
+    )
+    incoming = incoming.transpose(2, 1, 0, 3).reshape(2, slots, model_width)
+    arrived, arrived_grad = incoming[0], incoming[1]
     pre_act = jnp.dot(arrived, expert_in[0], preferred_element_type=jnp.float32)
     activated, gelu_slope = gelu_parts(pre_act)
     act_low = activated.astype(jnp.bfloat16)
     expert_part = jnp.dot(act_low, expert_out[0], preferred_element_type=jnp.float32)
-    returned = return_rows(expert_part, slot_target, experts, capacity).reshape(
-        length, 2, model_width
-    )
-    mixture = jnp.sum(gate_value[:, :, None] * returned.astype(jnp.float32), axis=1)
-    block_out = (residual_one + mixture).astype(jnp.bfloat16)
-    upstream = cotangent.astype(jnp.float32)
-    gate_grad = jnp.sum(upstream[:, None, :] * returned.astype(jnp.float32), axis=-1)
+    act_grad = jnp.einsum(
+        "rd,fd->rf", arrived_grad, expert_out[0], preferred_element_type=jnp.float32
+    )
+    pre_grad = (act_grad * gelu_slope).astype(jnp.bfloat16)
+    row_part = jnp.einsum("rf,df->rd", pre_grad, expert_in[0], preferred_element_type=jnp.float32)
+    parts = jnp.stack(
+        [
+            expert_part.astype(jnp.bfloat16).reshape(slots, shards, quarter),
+            row_part.astype(jnp.bfloat16).reshape(slots, shards, quarter),
+        ],
+        axis=2,
+    )
+    parts = parts.transpose(1, 0, 2, 3).reshape(shards, experts, capacity, 2 * quarter)
+    returned = give_back(parts, 3).reshape(slots, 2 * quarter)
+    rows = jnp.einsum("sp,sc->pc", place, returned, preferred_element_type=jnp.float32).reshape(
+        length, 2, 2, quarter
+    )
+    value_rows, grad_rows = rows[:, :, 0], rows[:, :, 1]
+    block_quarter = (
+        my_columns(residual_one) + jnp.sum(gate_value[:, :, None] * value_rows, axis=1)
+    ).astype(jnp.bfloat16)
+    gate_quarter = jnp.sum(my_columns(upstream)[:, None, :] * value_rows, axis=-1)
+    bundle = jnp.concatenate(
+        [block_quarter, jnp.sum(grad_rows, axis=1).astype(jnp.bfloat16)], axis=1
+    )
+    bundle_all, gate_all = exchange("shard", 4, (), (bundle, gate_quarter.T))
+    bundle_all = (
+        bundle_all.reshape(shards, length, 2, quarter)
+        .transpose(2, 1, 0, 3)
+        .reshape(2, length, model_width)
+    )
+    block_out = bundle_all[0]
+    gate_grad = jnp.sum(gate_all, axis=0).T
     logit_pair = gate_value * (gate_grad - jnp.sum(gate_value * gate_grad, axis=1, keepdims=True))
     logit_grad = jnp.sum(logit_pair[:, :, None] * route_hot, axis=1).astype(jnp.bfloat16)
     router_local = jnp.einsum(
-        "td,te->de", hidden_two, logit_grad, preferred_element_type=jnp.float32
+        "td,te->ed", hidden_two, logit_grad, preferred_element_type=jnp.float32
     )
     from_router = jnp.einsum("te,de->td", logit_grad, router, preferred_element_type=jnp.float32)
-    slot_grad = (
-        (gate_value[:, :, None] * upstream[:, None, :])
-        .astype(jnp.bfloat16)
-        .reshape(2 * length, model_width)
-    )
-    arrived_grad = send_rows(slot_grad, slot_target, experts, capacity)
-    act_grad = jnp.einsum(
-        "rd,fd->rf", arrived_grad, expert_out[0], preferred_element_type=jnp.float32
-    )
-    pre_grad = (act_grad * gelu_slope).astype(jnp.bfloat16)
     expert_out_local = jnp.einsum(
         "rf,rd->fd", act_low, arrived_grad, preferred_element_type=jnp.float32
     )
     expert_in_local = jnp.einsum("rd,rf->df", arrived, pre_grad, preferred_element_type=jnp.float32)
-    row_part = jnp.einsum("rf,df->rd", pre_grad, expert_in[0], preferred_element_type=jnp.float32)
-    row_grad = return_rows(row_part, slot_target, experts, capacity).reshape(length, 2, model_width)
-    hidden_two_grad = jnp.sum(row_grad.astype(jnp.float32), axis=1) + from_router
+    hidden_two_grad = bundle_all[1].astype(jnp.float32) + from_router
     gain_two_grad = jnp.sum(hidden_two_grad * normed_two, axis=0)
     residual_grad = upstream + norm_back(hidden_two_grad, normed_two, inverse_two, gain_two)
     residual_low = residual_grad.astype(jnp.bfloat16)
@@ -261,17 +502,21 @@
     hidden_one_part = jnp.einsum(
         "ctj,cdj->td", stacked, qkv_full, preferred_element_type=jnp.float32
     )
-    hidden_one_grad = lax.psum(hidden_one_part, "shard")
+    hidden_one_grad = sum_shards(hidden_one_part, 5)
     gain_one_grad = jnp.sum(hidden_one_grad * normed_one, axis=0)
     input_grad = residual_grad + norm_back(hidden_one_grad, normed_one, inverse_one, gain_one)
-    qkv_grad, out_grad, norm1_grad, norm2_grad, router_grad = (
-        lax.psum_scatter(qkv_local, "expert", scatter_dimension=1, tiled=True),
-        lax.psum_scatter(out_local, "expert", scatter_dimension=0, tiled=True),
-        lax.psum_scatter(gain_one_grad, "expert", scatter_dimension=0, tiled=True),
-        lax.psum_scatter(gain_two_grad, "expert", scatter_dimension=0, tiled=True),
-        lax.psum_scatter(router_local, "expert", scatter_dimension=0, tiled=True),
-    )
-    bias_grad = lax.psum(bias_local, "expert")
+    grads = jnp.concatenate([qkv_local, out_local[None]], axis=0).astype(jnp.bfloat16)
+    grads = grads.reshape(4, experts, -1, local_width).transpose(1, 0, 2, 3)
+    small_grads = jnp.concatenate([gain_one_grad[None], gain_two_grad[None], router_local], axis=0)
+    small_grads = small_grads.reshape(small_grads.shape[0], experts, -1).transpose(1, 0, 2)
+    grads_all, small_grads_all, bias_all = exchange(
+        "expert", 6, (grads, small_grads), (bias_local.T,)
+    )
+    grads_sum = jnp.sum(grads_all.astype(jnp.float32), axis=0)
+    small_sum = jnp.sum(small_grads_all, axis=0)
+    qkv_grad, out_grad = grads_sum[:3], grads_sum[3]
+    norm1_grad, norm2_grad, router_grad = small_sum[0], small_sum[1], small_sum[2:].T
+    bias_grad = jnp.sum(bias_all, axis=0).T
     return (
         block_out,
         input_grad,

time: 549 us -> 262 us (0.48)
  waiting for transfers between devices: 243 us -> 0 us
  blocking collectives: 181 us -> 0 us
  Pallas kernels: 0 us -> 161 us
  between operations: 16.2 us -> 1.64 us
  local copies, waits for them, and re-layouts: 40.9 us -> 55.1 us
  starting transfers between devices: 11.3 us -> 0 us
  other arithmetic: 24.9 us -> 18.3 us
    pallas_call x0 -> x7, Pallas kernels: none -> 161 us  [call(): pl.pallas_call(kernel, out_shape=out_shape, in_specs=[vmem] * len(operand...]
    all_gather x5 -> x0, blocking collectives: 101 us -> none  [the longest x1 37.2 us: local(): lax.all_gather(qkv_weight, 'expert', axis=1, tiled=True)]
    unnamed x9 -> x0, waiting for transfers between devices: 82.5 us -> none
    psum x2 -> x0, waiting for transfers between devices: 81.4 us -> none  [the longest x1 47.4 us: local(): residual_one = inputs + lax.psum(attn_part, 'shard')]
    reduce_scatter x3 -> x0, waiting for transfers between devices: 75.4 us -> none  [the longest x1 63.5 us: local(): lax.psum_scatter(out_local, 'expert', scatter_dimension=0, tiled=True)]
    all_to_all x2 -> x0, blocking collectives: 43.5 us -> none  [send_rows(): lax.all_to_all(buffer, 'expert', split_axis=0, concat_axis=0, tiled=True)]
    unnamed x2 -> x0, blocking collectives: 36 us -> none
    slice x1 -> x13, local copies, waits for them, and re-layouts: 0.21 us -> 21.3 us  [the longest x3 13.3 us: local(): arrived, arrived_grad = (incoming[0], incoming[1])]
  transfers between devices with their start and end apart: 9 -> 0, of which waited for: 7 -> 0; matrix products, arithmetic and copies ran while one was open for 10% -> 0% of each run, Pallas kernels for 0% -> 0%
where the time goes in v1:
time: 262 us; the launch traced here: 261 us
  Pallas kernels  161 us (61%)
  local copies, waits for them, and re-layouts  55.1 us (21%)
  matrix products  25 us (10%)
  other arithmetic  18.3 us (7%)
    pallas_call x7, Pallas kernels, call(): pl.pallas_call(kernel, out_shape=out_shape, in_specs=[vmem] * len(operand...  161 us
    slice x3, local copies, waits for them, and re-layouts, local(): arrived, arrived_grad = (incoming[0], incoming[1])  13.3 us
    slice x4, local copies, waits for them, and re-layouts, local(): qkv_full, out_full = (weights_all[:3], weights_all[3])  6.3 us
    unnamed x99, local copies, waits for them, and re-layouts  5.49 us

profile of v1, /device:TPU:11, one launch (start us, length us, event | category | flops | bytes accessed | tf_op | source)
XLA Modules:
  0.0 260.9 jit_solution(2981370554250565065)
XLA Ops:
  0.7 1.7 pad_maximum_fusion.refs_0_
  2.4 1.3 pad_maximum_fusion.5.refs_1_
  3.7 41.5 %shard_map.195 = (bf16[8,4,96,192]{3,2,1,0:T(8,128)(2,1)}, bf16[8,10,96]{2,1,0:T(8,128)(2,1)}) custom-call(bf16[4,96,192]{2,1,0:T(8,128)(2,1)} %pad_maximum_fusion.refs_0_, bf16[10,96]{1,0:T(8,128)(2,1)} %pad_maximum_fusion.5.refs_1_), custom_call_target="tpu_custom_call" | custom-call | tf_op jit(solution)/shard_map/pallas_call | solution.py:106
  45.2 0.8 fusion.63
  46.1 1.3 slice.111
  47.4 1.7 copy.126
  49.2 2.2 slice.86
  52.1 0.5 copy-done.43
  53.0 0.5 reshape.244
  54.5 1.0 slice.117
  55.6 0.8 copy-done.7
  56.4 1.0 convolution_convert_fusion.5.refs_0_
  57.3 13.1 %shard_map.196 = bf16[4,128,768]{2,1,0:T(8,128)(2,1)} custom-call(bf16[128,768]{1,0:T(8,128)(2,1)} %convolution_convert_fusion.5.refs_0_), custom_call_target="tpu_custom_call" | custom-call | tf_op jit(solution)/shard_map/pallas_call | solution.py:106
  70.5 1.3 convert_reduce_fusion.2
  73.0 0.5 copy-done.36
  73.9 0.6 copy-done.13
  75.6 0.6 reduce-window.6
  76.7 1.1 convolution_convert_fusion.4
  77.8 19.4 %shard_map.197 = bf16[4,8,64,384]{3,2,1,0:T(8,128)(2,1)} custom-call(bf16[8,64,384]{2,1,0:T(8,128)(2,1)} %bitcast.195), custom_call_target="tpu_custom_call" | custom-call | tf_op jit(solution)/shard_map/pallas_call | solution.py:106
  97.2 5.1 %reshape.251 = bf16[4,512,2,192]{3,2,1,0:T(2,128)(2,1)S(1)} reshape(bf16[4,8,64,384]{3,2,1,0:T(8,128)(2,1)} %shard_map.197) | data formatting | bytes 3145728 | tf_op jit(solution)/shard_map/reshape | solution.py:409
  102.3 4.2 %fusion.76 = (bf16[1,512,4,192]{3,0,1,2:T(2,128)(2,1)}, bf16[1,512,4,192]{3,0,1,2:T(2,128)(2,1)}) fusion(bf16[2,512,4,192]{3,0,1,2:T(2,128)(2,1)S(1)} %bitcast.163), kind=kLoop, calls=%fused_computation.148 | loop fusion | bytes 3145728 | tf_op jit(solution)/shard_map/slice | solution.py:413
  106.5 5.8 %copy.135 = bf16[1,512,4,192]{1,3,2,0:T(8,128)(2,1)} copy(bf16[1,512,4,192]{3,0,1,2:T(2,128)(2,1)} %get-tuple-element.77) | data formatting | bytes 1572864 | tf_op jit(solution)/shard_map/slice | solution.py:413
  112.3 3.6 %multiply_convert_fusion = (bf16[512,768]{1,0:T(8,128)(2,1)}, f32[512,768]{1,0:T(8,128)}) fusion(bf16[512,768]{0,1:T(8,128)(2,1)} %bitcast.168, bf16[1,768,768]{2,1,0:T(8,128)(2,1)S(1)} %copy-done), kind=kOutput, calls=%fused_computation.14 | convolution fusion | flops 605945856 | bytes 4325376 | tf_op jit(solution)/shard_map/dot_general | solution.py:414
  115.8 3.4 %copy.137 = bf16[1,512,4,192]{1,3,2,0:T(8,128)(2,1)} copy(bf16[1,512,4,192]{3,0,1,2:T(2,128)(2,1)S(1)} %copy-done.1) | data formatting | bytes 1572864 | tf_op jit(solution)/shard_map/slice | solution.py:413
  119.2 3.1 %fusion.6 = bf16[512,768]{1,0:T(8,128)(2,1)S(1)} fusion(f32[512,768]{1,0:T(8,128)} %get-tuple-element.86, bf16[512,768]{0,1:T(8,128)(2,1)} %bitcast.170, bf16[1,768,768]{2,1,0:T(8,128)(2,1)} %param.20), kind=kOutput, calls=%fused_computation.10 | convolution fusion | flops 607911936 | bytes 4325376 | tf_op jit(solution)/shard_map/rd,fd->rf/dot_general | solution.py:418
  122.3 0.9 copy-done.21
  123.2 0.8 convolution_convert_fusion.1
  124.3 3.2 %convolution_convert_fusion.2 = bf16[512,768]{1,0:T(8,128)(2,1)} fusion(bf16[512,768]{1,0:T(8,128)(2,1)} %get-tuple-element.85, bf16[1,768,768]{2,1,0:T(8,128)(2,1)} %param.20), kind=kOutput, calls=%fused_computation.19 | convolution fusion | flops 604372992 | bytes 2752512 | tf_op jit(solution)/shard_map/dot_general | solution.py:417
  127.4 1.4 copy.136
  128.8 1.3 maximum_bitcast_fusion
  130.1 4.8 %copy.139 = bf16[4,512,2,192]{3,2,1,0:T(2,128)(2,1)S(1)} copy(bf16[4,512,2,192]{1,3,0,2:T(8,128)(2,1)} %maximum_bitcast_fusion) | data formatting | bytes 3145728 | tf_op jit(solution)/shard_map/transpose | solution.py:430
  134.9 2.0 reshape.252.in_ref
  136.9 23.9 %shard_map.198 = bf16[8,64,384]{2,1,0:T(8,128)(2,1)} custom-call(bf16[4,8,64,384]{3,2,1,0:T(8,128)(2,1)} %reshape.252.in_ref), custom_call_target="tpu_custom_call" | custom-call | tf_op jit(solution)/shard_map/pallas_call | solution.py:106
  160.8 1.2 copy.140
  162.7 0.6 multiply_reduce_fusion.3
  163.7 0.7 pad_maximum_fusion.2.refs_0_
  164.4 8.9 %shard_map.199 = (bf16[4,128,384]{2,1,0:T(8,128)(2,1)}, f32[4,2,128]{2,1,0:T(2,128)}) custom-call(bf16[128,384]{1,0:T(8,128)(2,1)} %pad_maximum_fusion.2.refs_0_, f32[2,128]{1,0:T(2,128)} %bitcast.205), custom_call_target="tpu_custom_call" | custom-call | tf_op jit(solution)/shard_map/pallas_call | solution.py:106
  173.4 0.7 reduce_sum.227
  174.4 0.6 copy.152
  175.0 1.2 copy.144
  176.2 0.7 fusion.77
  177.6 0.8 convert_bitcast_fusion
  179.9 1.0 fusion.14.refs_0_
  181.0 12.7 %shard_map.200 = bf16[4,128,768]{2,1,0:T(8,128)(2,1)} custom-call(bf16[128,768]{1,0:T(8,128)(2,1)} %fusion.14.refs_0_), custom_call_target="tpu_custom_call" | custom-call | tf_op jit(solution)/shard_map/pallas_call | solution.py:106
  193.7 1.3 convert_reduce_fusion.1
  195.4 0.7 maximum_bitcast_fusion.2.refs_1_
  196.5 2.2 concatenate.38
  198.7 2.1 copy.151
  200.8 1.7 copy.150
  202.6 1.2 fusion.8
  203.8 1.4 maximum_bitcast_fusion.1.refs_0_
  205.8 0.5 reshape.258
  206.4 0.8 fusion.46.refs_2_
  207.2 41.3 %shard_map.201 = (bf16[8,4,96,192]{3,2,1,0:T(8,128)(2,1)}, f32[8,10,96]{2,1,0:T(8,128)}, f32[8,3,32]{2,1,0:T(4,128)}) custom-call(bf16[8,4,96,192]{3,2,1,0:T(8,128)(2,1)} %maximum_bitcast_fusion.1.refs_0_, f32[8,10,96]{2,1,0:T(8,128)} %maximum_bitcast_fusion.2.refs_1_, f32[3,32]{1,0:T(4,128)} %fusion.46.refs_2_), custom_call_target="tpu_custom_call" | custom-call | tf_op jit(solution)/shard_map/pallas_call | solution.py:106
  248.5 1.8 convert_reduce_fusion
  250.3 0.7 slice.129
  251.1 0.6 slice_bitcast_fusion.1
  251.7 0.6 slice_bitcast_fusion.2
  252.3 0.5 slice_bitcast_fusion.3
  252.8 0.6 reduce_sum.239
  253.4 3.4 %convolution_bitcast_fusion.1 = f32[1,768,768]{2,1,0:T(8,128)} fusion(bf16[512,768]{0,1:T(8,128)(2,1)S(1)} %bitcast.169, bf16[512,768]{1,0:T(8,128)(2,1)} %copy-done.21), kind=kOutput, calls=%fused_computation.4 | convolution fusion | flops 603979776 | bytes 3932160 | tf_op jit(solution)/shard_map/rd,rf->df/dot_general | solution.py:460
  256.9 2.2 convolution_bitcast_fusion
  259.1 0.9 fusion.34
  260.1 0.8 copy.154
  (171 shorter events, 10.1 us)
Async XLA Ops:
  0.6 111.6 %copy-start = (bf16[1,768,768]{2,1,0:T(8,128)(2,1)S(1)}, bf16[1,768,768]{2,1,0:T(8,128)(2,1)}, u32[]{:S(2)}) copy-start(bf16[1,768,768]{2,1,0:T(8,128)(2,1)} %param.19) | copy-start | bytes 3538948
  49.2 2.2 copy-start.4
  49.2 2.9 %copy-start.45 = (s32[31]{0:T(128)S(1)}, s32[31]{0:T(128)}, u32[]{:S(2)}) copy-start(s32[31]{0:T(128)} %constant.50.clone) | copy-start | bytes 376
  49.2 3.5 %copy-start.42 = (f32[32,3]{0,1:T(4,128)S(1)}, f32[32,3]{0,1:T(4,128)}, u32[]{:S(2)}) copy-start(f32[32,3]{0,1:T(4,128)} %param.18) | copy-start | bytes 1156
  51.4 2.2 copy-start.5
  51.5 2.2 copy-start.34
  52.0 2.0 copy-start.23
  52.0 2.0 copy-start.25
  52.0 2.3 copy-start.27
  52.1 0.5 copy-start.43
  54.3 16.2 %copy-start.15 = (f32[3,128,128]{1,2,0:T(8,128)}, f32[3,128,128]{1,2,0:T(8,128)S(1)}, u32[]{:S(2)}) copy-start(f32[3,128,128]{1,2,0:T(8,128)S(1)} %fusion.20) | copy-start | bytes 589828
  54.5 124.2 %copy-start.22 = (bf16[3,64,128]{2,1,0:T(8,128)(2,1)}, bf16[3,64,128]{2,1,0:T(8,128)(2,1)S(1)}, u32[]{:S(2)}) copy-start(bf16[3,64,128]{2,1,0:T(8,128)(2,1)S(1)} %convolution_convert_fusion.8) | copy-start | bytes 147460
  55.6 0.8 copy-start.7
  70.5 1.7 copy-start.31
  70.5 2.4 copy-start.33
  70.5 3.3 %copy-start.18 = (bf16[128,768]{1,0:T(8,128)(2,1)S(1)}, bf16[128,768]{1,0:T(8,128)(2,1)}, u32[]{:S(2)}) copy-start(bf16[128,768]{1,0:T(8,128)(2,1)} %param.22) | copy-start | bytes 589828
  72.0 3.0 %copy-start.2 = (f32[128,768]{1,0:T(8,128)}, f32[128,768]{1,0:T(8,128)S(1)}, u32[]{:S(2)}) copy-start(f32[128,768]{1,0:T(8,128)S(1)} %get-tuple-element.75) | copy-start | bytes 1179652
  72.0 0.6 copy-start.38
  72.2 3.1 %copy-start.11 = (bf16[128,768]{1,0:T(8,128)(2,1)}, bf16[128,768]{1,0:T(8,128)(2,1)S(1)}, u32[]{:S(2)}) copy-start(bf16[128,768]{1,0:T(8,128)(2,1)S(1)} %multiply_convert_fusion.1) | copy-start | bytes 589828
  73.0 0.5 copy-start.36
  73.9 0.7 copy-start.13
  76.7 1.1 copy-start.40
  112.3 3.6 %copy-start.1 = (bf16[1,512,4,192]{3,0,1,2:T(2,128)(2,1)S(1)}, bf16[1,512,4,192]{3,0,1,2:T(2,128)(2,1)}, u32[]{:S(2)}) copy-start(bf16[1,512,4,192]{3,0,1,2:T(2,128)(2,1)} %get-tuple-element.76) | copy-start | bytes 2359300
  122.3 0.9 copy-start.21
  136.9 25.1 %copy-start.41 = (s32[256]{0:T(256)S(1)}, s32[256]{0:T(256)}, u32[]{:S(2)}) copy-start(s32[256]{0:T(256)} %copy-done.40) | copy-start | bytes 3076
  160.7 1.9 copy-start.14
  160.8 2.7 %copy-start.3 = (f32[128,768]{1,0:T(8,128)S(1)}, f32[128,768]{1,0:T(8,128)}, u32[]{:S(2)}) copy-start(f32[128,768]{1,0:T(8,128)} %copy-done.2) | copy-start | bytes 1179652
  162.1 11.9 %copy-start.37 = (f32[128]{0:T(128)S(1)}, f32[128]{0:T(128)}, u32[]{:S(2)}) copy-start(f32[128]{0:T(128)} %copy-done.36) | copy-start | bytes 1540
  162.2 12.0 %copy-start.12 = (bf16[128,768]{1,0:T(8,128)(2,1)S(1)}, bf16[128,768]{1,0:T(8,128)(2,1)}, u32[]{:S(2)}) copy-start(bf16[128,768]{1,0:T(8,128)(2,1)} %copy-done.11) | copy-start | bytes 589828
  174.3 2.9 %copy-start.39 = (f32[128]{0:T(128)S(1)}, f32[128]{0:T(128)}, u32[]{:S(2)}) copy-start(f32[128]{0:T(128)} %copy-done.38) | copy-start | bytes 1540
  176.2 1.3 copy-start.19
  177.2 1.3 copy-start.8
  177.2 1.6 copy-start.16
  177.6 1.5 copy-start.28
  177.6 1.7 copy-start.26
  177.6 1.9 copy-start.24
  178.4 1.5 copy-start.6
  179.9 15.1 %copy-start.35 = (f32[128]{0:T(128)S(1)}, f32[128]{0:T(128)}, u32[]{:S(2)}) copy-start(f32[128]{0:T(128)} %copy-done.34) | copy-start | bytes 1540
  181.0 14.4 %copy-start.29 = (f32[8,8,96]{2,0,1:T(8,128)S(1)}, f32[8,8,96]{2,0,1:T(8,128)}, u32[]{:S(2)}) copy-start(f32[8,8,96]{2,0,1:T(8,128)} %copy.152) | copy-start | bytes 73732
  205.4 1.0 copy-start.44
  248.5 3.2 %copy-start.30 = (f32[8,10,96]{2,1,0:T(8,128)S(1)}, f32[8,10,96]{2,1,0:T(8,128)}, u32[]{:S(2)}) copy-start(f32[8,10,96]{2,1,0:T(8,128)} %get-tuple-element.22) | copy-start | bytes 92164
  248.5 4.3 %copy-start.32 = (f32[8,3,32]{2,1,0:T(4,128)S(1)}, f32[8,3,32]{2,1,0:T(4,128)}, u32[]{:S(2)}) copy-start(f32[8,3,32]{2,1,0:T(4,128)} %get-tuple-element.23) | copy-start | bytes 9220
  248.5 4.9 %copy-start.9 = (bf16[1,512,4,192]{1,3,2,0:T(8,128)(2,1)S(1)}, bf16[1,512,4,192]{1,3,2,0:T(8,128)(2,1)}, u32[]{:S(2)}) copy-start(bf16[1,512,4,192]{1,3,2,0:T(8,128)(2,1)} %copy.135) | copy-start | bytes 2359300
  253.4 3.4 %copy-start.10 = (bf16[1,512,4,192]{1,3,2,0:T(8,128)(2,1)S(1)}, bf16[1,512,4,192]{1,3,2,0:T(8,128)(2,1)}, u32[]{:S(2)}) copy-start(bf16[1,512,4,192]{1,3,2,0:T(8,128)(2,1)} %copy.137) | copy-start | bytes 2359300
  253.4 3.4 %copy-start.20 = (bf16[512,768]{1,0:T(8,128)(2,1)S(1)}, bf16[512,768]{1,0:T(8,128)(2,1)}, u32[]{:S(2)}) copy-start(bf16[512,768]{1,0:T(8,128)(2,1)} %get-tuple-element.85) | copy-start | bytes 2359300
  256.9 3.2 %copy-start.17 = (bf16[1,128,4,192]{1,3,0,2:T(8,128)(2,1)S(1)}, bf16[1,128,4,192]{1,3,0,2:T(8,128)(2,1)}, u32[]{:S(2)}) copy-start(bf16[1,128,4,192]{1,3,0,2:T(8,128)(2,1)} %get-tuple-element.79) | copy-start | bytes 589828

commit v2 on v1

--- a/solution.py
+++ b/solution.py
@@ -271,36 +271,183 @@
             if step < experts - 1:
                 copy = remote(
                     ready.at[step],
-                    out_ref.at[me],
+                    out_ref.at[shard, me],
                     sent.at[3, step],
                     arrived.at[3, step],
                     "expert",
                     peer,
                 )
             else:
-                copy = pltpu.make_async_copy(ready.at[step], out_ref.at[me], own_sem)
+                copy = pltpu.make_async_copy(ready.at[step], out_ref.at[shard, me], own_sem)
             copy.start()
             last.append(copy)
-        for copy in near + far:
+        side, over, rest = [], [], []
+        for step in range(experts):
+            origin = lax.rem(me + 2 * experts - step - 1, experts)
+            if step < experts - 1:
+                last[step].wait_recv()
+            else:
+                last[step].wait()
+            block = out_ref.at[shard, origin]
+            copy = remote(block, block, sent.at[5, step], arrived.at[5, step], "shard", across)
+            copy.start()
+            over.append(copy)
+            copy = remote(block, block, sent.at[4, step], arrived.at[4, step], "shard", beside)
+            copy.start()
+            side.append(copy)
+        for step in range(experts):
+            origin = lax.rem(me + 2 * experts - step - 1, experts)
+            over[step].wait_recv()
+            block = out_ref.at[across, origin]
+            copy = remote(block, block, sent.at[6, step], arrived.at[6, step], "shard", beside)
+            copy.start()
+            rest.append(copy)
+        for copy in near + far + last[: experts - 1] + over:
             copy.wait_send()
-        for copy in last:
+        for copy in side + rest:
             copy.wait()
 
     return call(
         kernel,
-        jax.ShapeDtypeStruct(block_shape, jnp.bfloat16),
+        jax.ShapeDtypeStruct(parts.shape, jnp.bfloat16),
         [
             pltpu.VMEM((2,) + block_shape, jnp.bfloat16),
             pltpu.VMEM(block_shape, jnp.float32),
             pltpu.VMEM(block_shape, jnp.bfloat16),
             pltpu.VMEM(block_shape, jnp.bfloat16),
             pltpu.VMEM(block_shape, jnp.bfloat16),
-            DMA((4, experts)),
-            DMA((4, experts)),
+            DMA((7, experts)),
+            DMA((7, experts)),
             DMA,
         ],
         collective,
         (parts,),
+    )
+
+
+def gather_pairs(operands, collective):
+    count = lax.axis_size("expert")
+    half = count // 2
+    total = len(operands)
+
+    def kernel(*refs):
+        ins, outs = refs[:total], refs[total : 2 * total]
+        sent, arrived, own_sem = refs[2 * total :]
+        me = lax.axis_index("expert")
+        mate = me + 1 - 2 * lax.rem(me, 2)
+        column = [lax.rem(me + 2 * step, count) for step in range(1, half)]
+        greet([("expert", peer) for peer in column + [mate]])
+        first, second = [], []
+        for step in range(1, half):
+            for index in range(total):
+                copy = remote(
+                    ins[index],
+                    outs[index].at[me],
+                    sent.at[0, index, step],
+                    arrived.at[0, index, step],
+                    "expert",
+                    column[step - 1],
+                )
+                copy.start()
+                first.append(copy)
+        own = []
+        for index in range(total):
+            copy = remote(
+                ins[index],
+                outs[index].at[me],
+                sent.at[1, index, 0],
+                arrived.at[1, index, 0],
+                "expert",
+                mate,
+            )
+            copy.start()
+            second.append(copy)
+            copy = pltpu.make_async_copy(ins[index], outs[index].at[me], own_sem.at[index])
+            copy.start()
+            own.append(copy)
+        for step in range(1, half):
+            origin = lax.rem(me + count - 2 * step, count)
+            for index in range(total):
+                first[(step - 1) * total + index].wait_recv()
+                block = outs[index].at[origin]
+                copy = remote(
+                    block,
+                    block,
+                    sent.at[1, index, step],
+                    arrived.at[1, index, step],
+                    "expert",
+                    mate,
+                )
+                copy.start()
+                second.append(copy)
+        for copy in first:
+            copy.wait_send()
+        for copy in second + own:
+            copy.wait()
+
+    out_shape = [jax.ShapeDtypeStruct((count,) + x.shape, x.dtype) for x in operands]
+    scratch = [DMA((2, total, half)), DMA((2, total, half)), DMA((total,))]
+    return call(kernel, out_shape, scratch, collective, operands)
+
+
+def reduce_pairs(spread, collective):
+    count = spread.shape[0]
+    half = count // 2
+    shape = (half,) + spread.shape[1:]
+    order = list(range(1, half)) + [0]
+
+    def kernel(in_ref, out_ref, pair, ready, sent, arrived):
+        me = lax.axis_index("expert")
+        mate = me + 1 - 2 * lax.rem(me, 2)
+        column = [lax.rem(me + 2 * step, count) for step in range(half)]
+        greet([("expert", peer) for peer in column[1:] + [mate]])
+        first, second = [], []
+        for step in order:
+            copy = remote(
+                in_ref.at[lax.rem(mate + 2 * step, count)],
+                pair.at[step],
+                sent.at[0, step],
+                arrived.at[0, step],
+                "expert",
+                mate,
+            )
+            copy.start()
+            first.append(copy)
+        for position, step in enumerate(order):
+            first[position].wait_recv()
+            value = (
+                in_ref[column[step]].astype(jnp.float32) + pair[step].astype(jnp.float32)
+            ).astype(jnp.bfloat16)
+            if step == 0:
+                out_ref[0] = value
+            else:
+                ready[step] = value
+                copy = remote(
+                    ready.at[step],
+                    out_ref.at[step],
+                    sent.at[1, step],
+                    arrived.at[1, step],
+                    "expert",
+                    column[step],
+                )
+                copy.start()
+                second.append(copy)
+        for copy in first:
+            copy.wait_send()
+        for copy in second:
+            copy.wait()
+
+    return call(
+        kernel,
+        jax.ShapeDtypeStruct(shape, spread.dtype),
+        [
+            pltpu.VMEM(shape, spread.dtype),
+            pltpu.VMEM(shape, spread.dtype),
+            DMA((2, half)),
+            DMA((2, half)),
+        ],
+        collective,
+        (spread,),
     )
 
 
@@ -328,10 +475,10 @@
     score_scale = 1.0 / math.sqrt(HEAD_DIM)
     shards = lax.axis_size("shard")
     shard = lax.axis_index("shard")
-    quarter = model_width // shards
+    rows = capacity // shards
     small = jnp.concatenate([norm1_gain[None], norm2_gain[None], router_weight.T], axis=0)
     weights = jnp.concatenate([qkv_weight, out_weight[None]], axis=0)
-    weights_all, small_all = exchange("expert", 0, (), (weights, small))
+    weights_all, small_all = gather_pairs((weights, small), 0)
     weights_all = weights_all.transpose(1, 0, 2, 3).reshape(4, model_width, -1)
     small_all = small_all.transpose(1, 0, 2).reshape(-1, model_width)
     qkv_full, out_full = weights_all[:3], weights_all[3]
@@ -388,29 +535,29 @@
     slot_target = flat_routes * capacity + slot_index
     upstream = cotangent.astype(jnp.float32)
 
-    def my_columns(matrix):
-        return lax.dynamic_slice_in_dim(matrix, shard * quarter, quarter, axis=1)
-
     slots = experts * capacity
-    place = (
-        lax.broadcasted_iota(jnp.int32, (slots, 2 * length), 0) == slot_target[None, :]
+    target_pair = slot_target.reshape(length, 2)
+    position = lax.broadcasted_iota(jnp.int32, (slots, length), 0)
+    slot_id = (
+        (position // rows) % experts * capacity
+        + position // (rows * experts) * rows
+        + position % rows
+    )
+    place = [(slot_id == target_pair[:, k][None, :]).astype(jnp.bfloat16) for k in range(2)]
+    mine = [lax.dynamic_slice_in_dim(p, shard * rows * experts, rows * experts) for p in place]
+    slot_grad = [(gate_value[:, k : k + 1] * upstream).astype(jnp.bfloat16) for k in range(2)]
+    outgoing = jnp.concatenate(
+        [
+            jnp.dot(mine[0] + mine[1], hidden_two, preferred_element_type=jnp.float32),
+            jnp.dot(mine[0], slot_grad[0], preferred_element_type=jnp.float32)
+            + jnp.dot(mine[1], slot_grad[1], preferred_element_type=jnp.float32),
+        ],
+        axis=1,
     ).astype(jnp.bfloat16)
-    hidden_rows = jnp.repeat(my_columns(hidden_two), 2, axis=0)
-    slot_grad = (
-        (gate_value[:, :, None] * my_columns(upstream)[:, None, :])
-        .astype(jnp.bfloat16)
-        .reshape(2 * length, quarter)
-    )
-    outgoing = jnp.dot(
-        place,
-        jnp.concatenate([hidden_rows, slot_grad], axis=1),
-        preferred_element_type=jnp.float32,
-    ).astype(jnp.bfloat16)
-    incoming = dispatch(outgoing.reshape(experts, capacity, 2 * quarter), 2).reshape(
-        shards, slots, 2, quarter
-    )
-    incoming = incoming.transpose(2, 1, 0, 3).reshape(2, slots, model_width)
-    arrived, arrived_grad = incoming[0], incoming[1]
+    incoming = dispatch(outgoing.reshape(experts, rows, 2 * model_width), 2).reshape(
+        slots, 2 * model_width
+    )
+    arrived, arrived_grad = incoming[:, :model_width], incoming[:, model_width:]
     pre_act = jnp.dot(arrived, expert_in[0], preferred_element_type=jnp.float32)
     activated, gelu_slope = gelu_parts(pre_act)
     act_low = activated.astype(jnp.bfloat16)
@@ -420,34 +567,18 @@
     )
     pre_grad = (act_grad * gelu_slope).astype(jnp.bfloat16)
     row_part = jnp.einsum("rf,df->rd", pre_grad, expert_in[0], preferred_element_type=jnp.float32)
-    parts = jnp.stack(
-        [
-            expert_part.astype(jnp.bfloat16).reshape(slots, shards, quarter),
-            row_part.astype(jnp.bfloat16).reshape(slots, shards, quarter),
-        ],
-        axis=2,
-    )
-    parts = parts.transpose(1, 0, 2, 3).reshape(shards, experts, capacity, 2 * quarter)
-    returned = give_back(parts, 3).reshape(slots, 2 * quarter)
-    rows = jnp.einsum("sp,sc->pc", place, returned, preferred_element_type=jnp.float32).reshape(
-        length, 2, 2, quarter
-    )
-    value_rows, grad_rows = rows[:, :, 0], rows[:, :, 1]
-    block_quarter = (
-        my_columns(residual_one) + jnp.sum(gate_value[:, :, None] * value_rows, axis=1)
+    parts = jnp.concatenate(
+        [expert_part.astype(jnp.bfloat16), row_part.astype(jnp.bfloat16)], axis=1
+    ).reshape(shards, experts, rows, 2 * model_width)
+    returned = give_back(parts, 3).reshape(slots, 2 * model_width)
+    pair_rows = [
+        jnp.einsum("sp,sc->pc", p, returned, preferred_element_type=jnp.float32) for p in place
+    ]
+    values = [r[:, :model_width] for r in pair_rows]
+    block_out = (
+        residual_one + gate_value[:, 0:1] * values[0] + gate_value[:, 1:2] * values[1]
     ).astype(jnp.bfloat16)
-    gate_quarter = jnp.sum(my_columns(upstream)[:, None, :] * value_rows, axis=-1)
-    bundle = jnp.concatenate(
-        [block_quarter, jnp.sum(grad_rows, axis=1).astype(jnp.bfloat16)], axis=1
-    )
-    bundle_all, gate_all = exchange("shard", 4, (), (bundle, gate_quarter.T))
-    bundle_all = (
-        bundle_all.reshape(shards, length, 2, quarter)
-        .transpose(2, 1, 0, 3)
-        .reshape(2, length, model_width)
-    )
-    block_out = bundle_all[0]
-    gate_grad = jnp.sum(gate_all, axis=0).T
+    gate_grad = jnp.stack([jnp.sum(upstream * v, axis=-1) for v in values], axis=1)
     logit_pair = gate_value * (gate_grad - jnp.sum(gate_value * gate_grad, axis=1, keepdims=True))
     logit_grad = jnp.sum(logit_pair[:, :, None] * route_hot, axis=1).astype(jnp.bfloat16)
     router_local = jnp.einsum(
@@ -458,7 +589,7 @@
         "rf,rd->fd", act_low, arrived_grad, preferred_element_type=jnp.float32
     )
     expert_in_local = jnp.einsum("rd,rf->df", arrived, pre_grad, preferred_element_type=jnp.float32)
-    hidden_two_grad = bundle_all[1].astype(jnp.float32) + from_router
+    hidden_two_grad = pair_rows[0][:, model_width:] + pair_rows[1][:, model_width:] + from_router
     gain_two_grad = jnp.sum(hidden_two_grad * normed_two, axis=0)
     residual_grad = upstream + norm_back(hidden_two_grad, normed_two, inverse_two, gain_two)
     residual_low = residual_grad.astype(jnp.bfloat16)
@@ -509,9 +640,8 @@
     grads = grads.reshape(4, experts, -1, local_width).transpose(1, 0, 2, 3)
     small_grads = jnp.concatenate([gain_one_grad[None], gain_two_grad[None], router_local], axis=0)
     small_grads = small_grads.reshape(small_grads.shape[0], experts, -1).transpose(1, 0, 2)
-    grads_all, small_grads_all, bias_all = exchange(
-        "expert", 6, (grads, small_grads), (bias_local.T,)
-    )
+    grads_all = reduce_pairs(grads, 6)
+    small_grads_all, bias_all = exchange("expert", 4, (small_grads,), (bias_local.T,))
     grads_sum = jnp.sum(grads_all.astype(jnp.float32), axis=0)
     small_sum = jnp.sum(small_grads_all, axis=0)
     qkv_grad, out_grad = grads_sum[:3], grads_sum[3]

time: 262 us -> 230 us (0.88)
  local copies, waits for them, and re-layouts: 55.1 us -> 30 us
  Pallas kernels: 161 us -> 147 us
  other arithmetic: 18.3 us -> 23.1 us
    pallas_call x7, Pallas kernels: 161 us -> 147 us  [call(): pl.pallas_call(kernel, out_shape=out_shape, in_specs=[vmem] * len(operand...]
    slice x5 -> x1, local copies, waits for them, and re-layouts: 14.2 us -> 0.21 us  [the longest x3 13.3 us: local(): arrived, arrived_grad = (incoming[0], incoming[1])]
    reshape x4 -> x0, local copies, waits for them, and re-layouts: 7.34 us -> none  [the longest x1 5.11 us: local(): dispatch(outgoing.reshape(experts, capacity, 2 * quarter), 2)]
    transpose x1 -> x0, local copies, waits for them, and re-layouts: 4.78 us -> none  [local(): parts.transpose(1, 0, 2, 3).reshape(shards, experts, capacity, 2 * quarter)]
    dot_general x2 -> x5, matrix products: 1.43 us -> 4.44 us  [the longest x2 3.7 us: local(): jnp.einsum('sp,sc->pc', p, returned, preferred_element_type=jnp.float32)]
    unnamed x99 -> x168, local copies, waits for them, and re-layouts: 5.49 us -> 4.82 us
where the time goes in v2:
time: 230 us; the launch traced here: 228 us
  Pallas kernels  147 us (64%)
  local copies, waits for them, and re-layouts  30 us (13%)
  matrix products  26.4 us (11%)
  other arithmetic  23.1 us (10%)
    pallas_call x7, Pallas kernels, call(): pl.pallas_call(kernel, out_shape=out_shape, in_specs=[vmem] * len(operand...  147 us
    slice x4, local copies, waits for them, and re-layouts, local(): qkv_full, out_full = (weights_all[:3], weights_all[3])  6.3 us
    concatenate x2, local copies, waits for them, and re-layouts, local(): jnp.concatenate([qkv_local, out_local[None]], axis=0).astype(jnp.bfloat16)  5.95 us
    unnamed x168, local copies, waits for them, and re-layouts  4.82 us

profile of v2, /device:TPU:11, one launch (start us, length us, event | category | flops | bytes accessed | tf_op | source)
XLA Modules:
  0.0 228.0 jit_solution(13448975112197966)
XLA Ops:
  0.7 1.7 pad_maximum_fusion.2.refs_0_
  2.4 1.3 pad_maximum_fusion.6.refs_1_
  3.7 27.4 %shard_map.195 = (bf16[8,4,96,192]{3,2,1,0:T(8,128)(2,1)}, bf16[8,10,96]{2,1,0:T(8,128)(2,1)}) custom-call(bf16[4,96,192]{2,1,0:T(8,128)(2,1)} %pad_maximum_fusion.2.refs_0_, bf16[10,96]{1,0:T(8,128)(2,1)} %pad_maximum_fusion.6.refs_1_), custom_call_target="tpu_custom_call" | custom-call | tf_op jit(solution)/shard_map/pallas_call | solution.py:106
  31.1 0.8 fusion.79
  32.0 1.3 slice.125
  33.3 1.7 copy.85
  35.1 2.2 slice.96
  37.4 0.5 fusion.22
  38.4 0.5 reshape.216
  40.0 1.0 slice.131
  41.0 0.7 copy-done.4
  41.8 1.0 convolution_convert_fusion.5.refs_0_
  42.7 13.8 %shard_map.196 = bf16[4,128,768]{2,1,0:T(8,128)(2,1)} custom-call(bf16[128,768]{1,0:T(8,128)(2,1)} %convolution_convert_fusion.5.refs_0_), custom_call_target="tpu_custom_call" | custom-call | tf_op jit(solution)/shard_map/pallas_call | solution.py:106
  56.6 1.3 convert_reduce_fusion.2
  59.1 0.5 copy-done.41
  60.0 0.6 reduce-window.6
  61.4 0.8 broadcast_compare_fusion
  63.2 0.8 pad_maximum_fusion.1.in_ref
  64.0 24.8 %shard_map.197 = bf16[4,8,16,1536]{3,2,1,0:T(8,128)(2,1)} custom-call(bf16[8,16,1536]{2,1,0:T(8,128)(2,1)} %pad_maximum_fusion.1.in_ref), custom_call_target="tpu_custom_call" | custom-call | tf_op jit(solution)/shard_map/pallas_call | solution.py:106
  88.8 2.1 multiply_convert_fusion
  91.0 1.1 fusion.6
  92.1 0.8 convolution_convert_fusion.1
  92.9 0.8 convolution_convert_fusion.2
  93.7 1.3 pad_maximum_fusion
  95.0 30.6 %shard_map.198 = bf16[4,8,16,1536]{3,2,1,0:T(8,128)(2,1)} custom-call(bf16[4,8,16,1536]{3,2,1,0:T(8,128)(2,1)} %bitcast.138), custom_call_target="tpu_custom_call" | custom-call | tf_op jit(solution)/shard_map/pallas_call | solution.py:106
  125.7 2.6 %fusion.101 = f32[128,1536]{1,0:T(8,128)S(1)} fusion(bf16[512,1536]{1,0:T(8,128)(2,1)} %bitcast.149, s32[128]{0:T(128)} %copy-done.68, s32[512]{0:T(512)} %copy-done.47, s32[512]{0:T(512)} %copy-done.49, pred[512]{0:T(512)(128)(4,1)} %copy-done.72, s32[512]{0:T(512)} %copy-done.43, s32[512]{0:T(512)} %copy-done.51, pred[512]{0:T(512)(128)(4,1)} %copy-done.70, ...), kind=kOutput, calls=%fused_computation.187 | convolution fusion | flops 202571776 | bytes 2373632 | tf_op jit(solution)/shard_map/sp,sc->pc/dot_general | solution.py:575
  128.5 1.1 fusion.100
  129.6 0.9 fusion.42
  130.6 0.6 copy-done.36
  131.2 0.8 fusion.104
  132.0 1.4 concatenate.54
  133.4 1.4 copy.98
  134.8 2.1 multiply_reduce_fusion
  137.0 0.8 convert_bitcast_fusion
  139.4 1.3 convolution_convert_fusion.7
  140.8 2.2 fusion.14.refs_0_
  143.0 12.8 %shard_map.199 = bf16[4,128,768]{2,1,0:T(8,128)(2,1)} custom-call(bf16[128,768]{1,0:T(8,128)(2,1)} %fusion.14.refs_0_), custom_call_target="tpu_custom_call" | custom-call | tf_op jit(solution)/shard_map/pallas_call | solution.py:106
  155.8 1.3 convert_reduce_fusion.1
  157.1 0.8 fusion.38
  158.0 1.4 maximum_bitcast_fusion.1.refs_0_
  159.4 1.3 rev.8
  160.7 1.1 copy.106
  162.1 0.9 slice.143
  163.0 2.3 %reshape.226 = f32[3,128,255]{2,1,0:T(8,128)} reshape(f32[3,32640]{1,0:T(4,128)} %slice.143) | data formatting | bytes 783360 | tf_op jit(solution)/shard_map/reshape | solution.py:62
  165.3 1.0 reduce_sum.220
  166.4 0.8 fusion.58.refs_1_
  167.2 7.7 %shard_map.201 = (f32[8,10,96]{2,1,0:T(8,128)}, f32[8,3,32]{2,1,0:T(4,128)}) custom-call(f32[8,10,96]{2,1,0:T(8,128)} %maximum_bitcast_fusion.1.refs_0_, f32[3,32]{1,0:T(4,128)} %fusion.58.refs_1_), custom_call_target="tpu_custom_call" | custom-call | tf_op jit(solution)/shard_map/pallas_call | solution.py:106
  174.9 0.9 reduce_sum.221
  175.7 0.6 slice_bitcast_fusion.1
  176.3 0.5 slice_bitcast_fusion.2
  176.8 1.3 reduce_sum.222
  178.2 1.4 fusion.7
  179.5 3.2 %concatenate.50 = bf16[3,8,96,192]{2,1,3,0:T(8,128)(2,1)} reshape(bf16[3,768,192]{1,2,0:T(8,128)(2,1)} %fusion.7) | data formatting | bytes 1769472 | tf_op jit(solution)/shard_map/concatenate | solution.py:639
  182.7 2.8 %copy.97 = bf16[3,8,96,192]{3,2,0,1:T(8,128)(2,1)} copy(bf16[3,8,96,192]{2,1,3,0:T(8,128)(2,1)} %concatenate.50) | data formatting | bytes 1769472 | tf_op jit(solution)/shard_map/concatenate | solution.py:639
  185.5 1.1 copy.96
  186.6 1.1 fusion.8
  187.7 2.7 %maximum_bitcast_fusion.in_ref = bf16[8,4,96,192]{3,2,1,0:T(8,128)(2,1)} fusion(bf16[1,8,96,192]{3,2,0,1:T(8,128)(2,1)S(1)} %fusion.8, bf16[3,8,96,192]{3,2,0,1:T(8,128)(2,1)} %copy.97), kind=kLoop, calls=%fused_computation.11 | loop fusion | flops 589824 | bytes 2359296 | tf_op jit(solution)/shard_map/transpose | solution.py:640
  190.3 29.5 %shard_map.200 = bf16[4,4,96,192]{3,2,1,0:T(8,128)(2,1)} custom-call(bf16[8,4,96,192]{3,2,1,0:T(8,128)(2,1)} %maximum_bitcast_fusion.in_ref), custom_call_target="tpu_custom_call" | custom-call | tf_op jit(solution)/shard_map/pallas_call | solution.py:106
  219.9 1.4 convert_reduce_fusion
  221.3 0.7 slice.141
  222.0 0.6 slice_bitcast_fusion
  222.6 2.2 convolution_bitcast_fusion.1
  224.9 2.2 convolution_bitcast_fusion
  227.1 0.9 fusion.37
  (222 shorter events, 6.9 us)
Async XLA Ops:
  0.6 88.1 %copy-start = (bf16[1,768,768]{2,1,0:T(8,128)(2,1)S(1)}, bf16[1,768,768]{2,1,0:T(8,128)(2,1)}, u32[]{:S(2)}) copy-start(bf16[1,768,768]{2,1,0:T(8,128)(2,1)} %param.19) | copy-start | bytes 3538948
  35.1 2.2 copy-start.2
  35.1 2.9 %copy-start.80 = (s32[31]{0:T(128)S(1)}, s32[31]{0:T(128)}, u32[]{:S(2)}) copy-start(s32[31]{0:T(128)} %constant.106.clone) | copy-start | bytes 376
  35.1 3.0 %copy-start.77 = (f32[32,3]{0,1:T(4,128)S(1)}, f32[32,3]{0,1:T(4,128)}, u32[]{:S(2)}) copy-start(f32[32,3]{0,1:T(4,128)} %param.18) | copy-start | bytes 1156
  37.3 1.7 copy-start.3
  37.4 1.7 copy-start.55
  37.9 1.5 copy-start.26
  37.9 1.5 copy-start.28
  37.9 1.8 copy-start.32
  38.1 1.1 copy-start.78
  39.7 16.8 %copy-start.12 = (f32[3,128,128]{1,2,0:T(8,128)}, f32[3,128,128]{1,2,0:T(8,128)S(1)}, u32[]{:S(2)}) copy-start(f32[3,128,128]{1,2,0:T(8,128)S(1)} %fusion.21) | copy-start | bytes 589828
  40.0 16.6 %copy-start.24 = (bf16[3,64,128]{2,1,0:T(8,128)(2,1)}, bf16[3,64,128]{2,1,0:T(8,128)(2,1)S(1)}, u32[]{:S(2)}) copy-start(bf16[3,64,128]{2,1,0:T(8,128)(2,1)S(1)} %convolution_convert_fusion.8) | copy-start | bytes 147460
  56.6 1.7 copy-start.37
  56.6 2.4 %copy-start.39 = (s32[128,2]{0,1:T(2,128)S(1)}, s32[128,2]{0,1:T(2,128)}, u32[]{:S(2)}) copy-start(s32[128,2]{0,1:T(2,128)} %param.21) | copy-start | bytes 3076
  56.6 5.8 %copy-start.8 = (bf16[128,768]{1,0:T(8,128)(2,1)S(1)}, bf16[128,768]{1,0:T(8,128)(2,1)}, u32[]{:S(2)}) copy-start(bf16[128,768]{1,0:T(8,128)(2,1)} %param.22) | copy-start | bytes 589828
  58.3 5.7 %copy-start.9 = (bf16[128,768]{1,0:T(8,128)(2,1)}, bf16[128,768]{1,0:T(8,128)(2,1)S(1)}, u32[]{:S(2)}) copy-start(bf16[128,768]{1,0:T(8,128)(2,1)S(1)} %multiply_convert_fusion.1) | copy-start | bytes 589828
  59.7 3.0 %copy-start.60 = (f32[128]{0:T(128)}, f32[128]{0:T(128)S(1)}, u32[]{:S(2)}) copy-start(f32[128]{0:T(128)S(1)} %get-tuple-element.41) | copy-start | bytes 1540
  59.7 4.3 %copy-start.58 = (f32[128]{0:T(128)}, f32[128]{0:T(128)S(1)}, u32[]{:S(2)}) copy-start(f32[128]{0:T(128)S(1)} %get-tuple-element.40) | copy-start | bytes 1540
  61.3 1.0 copy-start.66
  61.3 1.0 copy-start.68
  61.3 1.0 copy-start.43
  88.8 2.2 copy-start.1
  88.8 2.2 copy-start.76
  90.9 2.0 copy-start.16
  125.6 2.7 %copy-start.11 = (bf16[4,8,16,1536]{3,2,1,0:T(8,128)(2,1)S(1)}, bf16[4,8,16,1536]{3,2,1,0:T(8,128)(2,1)}, u32[]{:S(2)}) copy-start(bf16[4,8,16,1536]{3,2,1,0:T(8,128)(2,1)} %shard_map.198) | copy-start | bytes 4718596
  125.6 2.7 %copy-start.44 = (s32[512]{0:T(512)S(1)}, s32[512]{0:T(512)}, u32[]{:S(2)}) copy-start(s32[512]{0:T(512)} %copy-done.43) | copy-start | bytes 6148
  125.6 2.7 %copy-start.46 = (s32[512]{0:T(512)S(1)}, s32[512]{0:T(512)}, u32[]{:S(2)}) copy-start(s32[512]{0:T(512)} %copy-done.45) | copy-start | bytes 6148
  125.6 2.7 %copy-start.48 = (s32[512]{0:T(512)S(1)}, s32[512]{0:T(512)}, u32[]{:S(2)}) copy-start(s32[512]{0:T(512)} %copy-done.47) | copy-start | bytes 6148
  125.6 2.7 %copy-start.50 = (s32[512]{0:T(512)S(1)}, s32[512]{0:T(512)}, u32[]{:S(2)}) copy-start(s32[512]{0:T(512)} %copy-done.49) | copy-start | bytes 6148
  125.6 2.7 %copy-start.52 = (s32[512]{0:T(512)S(1)}, s32[512]{0:T(512)}, u32[]{:S(2)}) copy-start(s32[512]{0:T(512)} %copy-done.51) | copy-start | bytes 6148
  125.6 2.7 %copy-start.54 = (s32[512]{0:T(512)S(1)}, s32[512]{0:T(512)}, u32[]{:S(2)}) copy-start(s32[512]{0:T(512)} %copy-done.53) | copy-start | bytes 6148
  125.6 2.7 %copy-start.67 = (s32[128]{0:T(128)S(1)}, s32[128]{0:T(128)}, u32[]{:S(2)}) copy-start(s32[128]{0:T(128)} %copy-done.66) | copy-start | bytes 1540
  125.6 2.7 %copy-start.71 = (pred[512]{0:T(512)(128)(4,1)S(1)}, pred[512]{0:T(512)(128)(4,1)}, u32[]{:S(2)}) copy-start(pred[512]{0:T(512)(128)(4,1)} %copy-done.70) | copy-start | bytes 1540
  125.7 2.7 %copy-start.73 = (pred[512]{0:T(512)(128)(4,1)S(1)}, pred[512]{0:T(512)(128)(4,1)}, u32[]{:S(2)}) copy-start(pred[512]{0:T(512)(128)(4,1)} %copy-done.72) | copy-start | bytes 1540
  125.7 2.7 %copy-start.75 = (pred[512]{0:T(512)(128)(4,1)S(1)}, pred[512]{0:T(512)(128)(4,1)}, u32[]{:S(2)}) copy-start(pred[512]{0:T(512)(128)(4,1)} %copy-done.74) | copy-start | bytes 1540
  128.4 2.1 copy-start.14
  128.4 1.2 copy-start.59
  128.4 1.2 copy-start.61
  128.4 2.1 copy-start.42
  128.4 2.1 copy-start.63
  128.5 2.1 copy-start.40
  128.5 2.7 %copy-start.10 = (bf16[128,768]{1,0:T(8,128)(2,1)S(1)}, bf16[128,768]{1,0:T(8,128)(2,1)}, u32[]{:S(2)}) copy-start(bf16[128,768]{1,0:T(8,128)(2,1)} %copy-done.9) | copy-start | bytes 589828
  133.4 3.6 %copy-start.35 = (f32[768]{0:T(1024)S(1)}, f32[768]{0:T(1024)}, u32[]{:S(2)}) copy-start(f32[768]{0:T(1024)} %copy-done.34) | copy-start | bytes 9220
  133.4 3.6 %copy-start.65 = (f32[128]{0:T(128)S(1)}, f32[128]{0:T(128)}, u32[]{:S(2)}) copy-start(f32[128]{0:T(128)} %copy-done.64) | copy-start | bytes 1540
  134.8 3.0 %copy-start.5 = (bf16[1,8,96,192]{3,2,0,1:T(8,128)(2,1)S(1)}, bf16[1,8,96,192]{3,2,0,1:T(8,128)(2,1)}, u32[]{:S(2)}) copy-start(bf16[1,8,96,192]{3,2,0,1:T(8,128)(2,1)} %copy-done.4) | copy-start | bytes 884740
  136.9 1.6 copy-start.25
  136.9 1.7 copy-start.13
  136.9 1.9 copy-start.33
  137.0 2.1 copy-start.29
  137.0 2.3 %copy-start.27 = (bf16[1,128,192]{1,2,0:T(8,128)(2,1)S(1)}, bf16[1,128,192]{1,2,0:T(8,128)(2,1)}, u32[]{:S(2)}) copy-start(bf16[1,128,192]{1,2,0:T(8,128)(2,1)} %copy-done.26) | copy-start | bytes 147460
  139.2 3.7 %copy-start.20 = (bf16[3,64,128]{2,1,0:T(8,128)(2,1)}, bf16[3,64,128]{2,1,0:T(8,128)(2,1)S(1)}, u32[]{:S(2)}) copy-start(bf16[3,64,128]{2,1,0:T(8,128)(2,1)S(1)} %fusion.23) | copy-start | bytes 147460
  139.4 3.5 %copy-start.22 = (bf16[3,64,128]{2,1,0:T(8,128)(2,1)}, bf16[3,64,128]{2,1,0:T(8,128)(2,1)S(1)}, u32[]{:S(2)}) copy-start(bf16[3,64,128]{2,1,0:T(8,128)(2,1)S(1)} %fusion.24) | copy-start | bytes 147460
  140.7 2.2 copy-start.30
  140.8 16.3 %copy-start.56 = (f32[128]{0:T(128)S(1)}, f32[128]{0:T(128)}, u32[]{:S(2)}) copy-start(f32[128]{0:T(128)} %copy-done.55) | copy-start | bytes 1540
  143.0 15.0 %copy-start.38 = (f32[768]{0:T(1024)S(1)}, f32[768]{0:T(1024)}, u32[]{:S(2)}) copy-start(f32[768]{0:T(1024)} %get-tuple-element.18) | copy-start | bytes 9220
  161.8 4.6 %copy-start.79 = (s32[128]{0:T(128)S(1)}, s32[128]{0:T(128)}, u32[]{:S(2)}) copy-start(s32[128]{0:T(128)} %copy-done.78) | copy-start | bytes 1540
  161.8 16.3 %copy-start.21 = (bf16[3,64,128]{2,1,0:T(8,128)(2,1)S(1)}, bf16[3,64,128]{2,1,0:T(8,128)(2,1)}, u32[]{:S(2)}) copy-start(bf16[3,64,128]{2,1,0:T(8,128)(2,1)} %copy-done.20) | copy-start | bytes 147460
  161.8 16.3 %copy-start.23 = (bf16[3,64,128]{2,1,0:T(8,128)(2,1)S(1)}, bf16[3,64,128]{2,1,0:T(8,128)(2,1)}, u32[]{:S(2)}) copy-start(bf16[3,64,128]{2,1,0:T(8,128)(2,1)} %copy-done.22) | copy-start | bytes 147460
  161.8 16.3 %copy-start.31 = (bf16[3,64,128]{2,1,0:T(8,128)(2,1)S(1)}, bf16[3,64,128]{2,1,0:T(8,128)(2,1)}, u32[]{:S(2)}) copy-start(bf16[3,64,128]{2,1,0:T(8,128)(2,1)} %copy-done.30) | copy-start | bytes 147460
  161.8 16.3 %copy-start.57 = (f32[128]{0:T(128)S(1)}, f32[128]{0:T(128)}, u32[]{:S(2)}) copy-start(f32[128]{0:T(128)} %copy-done.55) | copy-start | bytes 1540
  219.9 2.8 %copy-start.19 = (bf16[512,768]{1,0:T(8,128)(2,1)S(1)}, bf16[512,768]{1,0:T(8,128)(2,1)}, u32[]{:S(2)}) copy-start(bf16[512,768]{1,0:T(8,128)(2,1)} %copy-done.18) | copy-start | bytes 2359300
  222.6 2.2 copy-start.17
  224.9 2.2 copy-start.69
  224.9 2.2 copy-start.7
  (17 other events, 14.2 us)

commit v3 on v2

--- a/solution.py
+++ b/solution.py
@@ -477,21 +477,22 @@
     shard = lax.axis_index("shard")
     rows = capacity // shards
     small = jnp.concatenate([norm1_gain[None], norm2_gain[None], router_weight.T], axis=0)
-    weights = jnp.concatenate([qkv_weight, out_weight[None]], axis=0)
+    weights = jnp.concatenate([qkv_weight[0], qkv_weight[1], qkv_weight[2], out_weight], axis=1)
     weights_all, small_all = gather_pairs((weights, small), 0)
-    weights_all = weights_all.transpose(1, 0, 2, 3).reshape(4, model_width, -1)
+    weights_all = weights_all.reshape(model_width, -1)
     small_all = small_all.transpose(1, 0, 2).reshape(-1, model_width)
-    qkv_full, out_full = weights_all[:3], weights_all[3]
+    local_width = out_weight.shape[1]
+    qkv_full, out_full = weights_all[:, : 3 * local_width], weights_all[:, 3 * local_width :]
     gain_low_one, gain_low_two, router = small_all[0], small_all[1], small_all[2:].T
     gain_one = gain_low_one.astype(jnp.float32)
     gain_two = gain_low_two.astype(jnp.float32)
     inputs = block_in.astype(jnp.float32)
     normed_one, inverse_one = normalize(inputs)
     hidden_one = (normed_one * gain_one).astype(jnp.bfloat16)
-    projected = jnp.einsum(
-        "td,cdj->ctj", hidden_one, qkv_full, preferred_element_type=jnp.float32
+    projected_flat = jnp.dot(
+        hidden_one, qkv_full, preferred_element_type=jnp.float32
     ).astype(jnp.bfloat16)
-    local_width = projected.shape[2]
+    projected = [projected_flat[:, c * local_width : (c + 1) * local_width] for c in range(3)]
     local_heads = local_width // HEAD_DIM
     queries = projected[0].reshape(length, local_heads, HEAD_DIM)
     keys_local = projected[1].reshape(length, local_heads, HEAD_DIM)
@@ -626,25 +627,31 @@
         jnp.einsum("hij,ihd->jhd", score_low, queries, preferred_element_type=jnp.float32)
         * score_scale
     ).astype(jnp.bfloat16)
-    stacked = jnp.stack([query_grad, key_grad, value_grad.astype(jnp.bfloat16)]).reshape(
-        3, length, local_width
-    )
-    qkv_local = jnp.einsum("td,ctj->cdj", hidden_one, stacked, preferred_element_type=jnp.float32)
-    hidden_one_part = jnp.einsum(
-        "ctj,cdj->td", stacked, qkv_full, preferred_element_type=jnp.float32
-    )
+    stacked = jnp.concatenate(
+        [
+            x.reshape(length, local_width)
+            for x in (query_grad, key_grad, value_grad.astype(jnp.bfloat16))
+        ],
+        axis=1,
+    )
+    qkv_local = jnp.einsum("td,tj->dj", hidden_one, stacked, preferred_element_type=jnp.float32)
+    hidden_one_part = jnp.einsum("tj,dj->td", stacked, qkv_full, preferred_element_type=jnp.float32)
     hidden_one_grad = sum_shards(hidden_one_part, 5)
     gain_one_grad = jnp.sum(hidden_one_grad * normed_one, axis=0)
     input_grad = residual_grad + norm_back(hidden_one_grad, normed_one, inverse_one, gain_one)
-    grads = jnp.concatenate([qkv_local, out_local[None]], axis=0).astype(jnp.bfloat16)
-    grads = grads.reshape(4, experts, -1, local_width).transpose(1, 0, 2, 3)
+    grads = jnp.concatenate(
+        [qkv_local.astype(jnp.bfloat16), out_local.astype(jnp.bfloat16)], axis=1
+    ).reshape(experts, -1, 4 * local_width)
     small_grads = jnp.concatenate([gain_one_grad[None], gain_two_grad[None], router_local], axis=0)
     small_grads = small_grads.reshape(small_grads.shape[0], experts, -1).transpose(1, 0, 2)
     grads_all = reduce_pairs(grads, 6)
     small_grads_all, bias_all = exchange("expert", 4, (small_grads,), (bias_local.T,))
     grads_sum = jnp.sum(grads_all.astype(jnp.float32), axis=0)
     small_sum = jnp.sum(small_grads_all, axis=0)
-    qkv_grad, out_grad = grads_sum[:3], grads_sum[3]
+    qkv_grad = jnp.stack(
+        [grads_sum[:, c * local_width : (c + 1) * local_width] for c in range(3)]
+    )
+    out_grad = grads_sum[:, 3 * local_width :]
     norm1_grad, norm2_grad, router_grad = small_sum[0], small_sum[1], small_sum[2:].T
     bias_grad = jnp.sum(bias_all, axis=0).T
     return (

time: 230 us -> 207 us (0.900)
  Pallas kernels: 147 us -> 133 us
  local copies, waits for them, and re-layouts: 30 us -> 16.3 us
  matrix products: 26.4 us -> 29.8 us
    pallas_call x7, Pallas kernels: 147 us -> 133 us  [call(): pl.pallas_call(kernel, out_shape=out_shape, in_specs=[vmem] * len(operand...]
    slice x7 -> x3, local copies, waits for them, and re-layouts: 7.26 us -> 0.97 us  [the longest x1 0.75 us: local(): out_grad = grads_sum[:, 3 * local_width:]]
    concatenate x2 -> x1, local copies, waits for them, and re-layouts: 5.95 us -> 2.37 us  [local(): jnp.concatenate([qkv_local.astype(jnp.bfloat16), out_local.astype(jnp.bfl...]
    transpose x1 -> x0, other arithmetic: 2.68 us -> none  [local(): grads = grads.reshape(4, experts, -1, local_width).transpose(1, 0, 2, 3)]
    unnamed x168 -> x150, local copies, waits for them, and re-layouts: 4.82 us -> 3.86 us
where the time goes in v3:
time: 207 us; the launch traced here: 204 us
  Pallas kernels  133 us (64%)
  matrix products  29.8 us (14%)
  other arithmetic  23.1 us (11%)
  local copies, waits for them, and re-layouts  16.3 us (8%)
    pallas_call x7, Pallas kernels, call(): pl.pallas_call(kernel, out_shape=out_shape, in_specs=[vmem] * len(operand...  133 us

profile of v3, /device:TPU:11, one launch (start us, length us, event | category | flops | bytes accessed | tf_op | source)
XLA Modules:
  0.0 204.4 jit_solution(12160111047744350231)
XLA Ops:
  0.7 0.9 slice_bitcast_fusion.5
  1.6 1.6 pad_maximum_fusion.4.refs_0_
  3.2 1.3 pad_maximum_fusion.8.refs_1_
  4.5 22.0 %shard_map.195 = (bf16[8,96,768]{2,1,0:T(8,128)(2,1)}, bf16[8,10,96]{2,1,0:T(8,128)(2,1)}) custom-call(bf16[96,768]{1,0:T(8,128)(2,1)} %pad_maximum_fusion.4.refs_0_, bf16[10,96]{1,0:T(8,128)(2,1)} %pad_maximum_fusion.8.refs_1_), custom_call_target="tpu_custom_call" | custom-call | tf_op jit(solution)/shard_map/pallas_call | solution.py:106
  26.5 0.8 fusion.79
  27.4 1.0 fusion.37
  28.4 1.9 convolution_convert_fusion.7
  30.8 0.5 reshape.221
  32.4 2.1 %convolution_convert_fusion.5.refs_0_ = bf16[128,768]{1,0:T(8,128)(2,1)} fusion(bf16[128,192]{0,1:T(8,128)(2,1)S(1)} %bitcast.132, bf16[768,768]{1,0:T(8,128)(2,1)} %bitcast.129), kind=kOutput, calls=%fused_computation.30 | convolution fusion | flops 37847040 | bytes 638976 | tf_op jit(solution)/shard_map/tc,mc->tm/dot_general | solution.py:523
  34.5 13.8 %shard_map.196 = bf16[4,128,768]{2,1,0:T(8,128)(2,1)} custom-call(bf16[128,768]{1,0:T(8,128)(2,1)} %convolution_convert_fusion.5.refs_0_), custom_call_target="tpu_custom_call" | custom-call | tf_op jit(solution)/shard_map/pallas_call | solution.py:106
  48.3 1.3 convert_reduce_fusion.1
  50.1 0.3 copy-done.56
  50.5 0.6 reduce-window.6
  52.0 0.8 broadcast_compare_fusion
  53.6 0.5 copy-done.54
  54.1 0.3 fusion.49
  54.4 0.3 copy-done.52
  54.7 0.3 fusion.12
  55.0 0.8 pad_maximum_fusion.2.in_ref
  55.7 23.7 %shard_map.197 = bf16[4,8,16,1536]{3,2,1,0:T(8,128)(2,1)} custom-call(bf16[8,16,1536]{2,1,0:T(8,128)(2,1)} %pad_maximum_fusion.2.in_ref), custom_call_target="tpu_custom_call" | custom-call | tf_op jit(solution)/shard_map/pallas_call | solution.py:106
  79.5 2.1 %multiply_convert_fusion = (bf16[512,768]{1,0:T(8,128)(2,1)S(1)}, f32[512,768]{1,0:T(8,128)S(1)}) fusion(bf16[1,768,768]{2,1,0:T(8,128)(2,1)S(1)} %copy-done, bf16[512,1536]{1,0:T(8,128)(2,1)} %bitcast.116), kind=kOutput, calls=%fused_computation.12 | convolution fusion | flops 605945856 | bytes 4325376 | tf_op jit(solution)/shard_map/dot_general | solution.py:562
  81.7 1.1 fusion.6
  82.8 0.8 convolution_convert_fusion.1
  83.6 0.8 convolution_convert_fusion.2
  84.4 1.3 pad_maximum_fusion
  85.7 30.5 %shard_map.198 = bf16[4,8,16,1536]{3,2,1,0:T(8,128)(2,1)} custom-call(bf16[4,8,16,1536]{3,2,1,0:T(8,128)(2,1)} %bitcast.115), custom_call_target="tpu_custom_call" | custom-call | tf_op jit(solution)/shard_map/pallas_call | solution.py:106
  116.3 2.6 %fusion.101 = f32[128,1536]{1,0:T(8,128)S(1)} fusion(bf16[512,1536]{1,0:T(8,128)(2,1)} %bitcast.123, s32[128]{0:T(128)} %copy-done.59, s32[512]{0:T(512)} %copy-done.39, s32[512]{0:T(512)} %copy-done.41, pred[512]{0:T(512)(128)(4,1)} %copy-done.63, s32[512]{0:T(512)} %copy-done.35, s32[512]{0:T(512)} %copy-done.43, pred[512]{0:T(512)(128)(4,1)} %copy-done.61, ...), kind=kOutput, calls=%fused_computation.192 | convolution fusion | flops 202571776 | bytes 2373632 | tf_op jit(solution)/shard_map/sp,sc->pc/dot_general | solution.py:576
  119.1 1.1 fusion.100
  120.3 0.9 fusion.40
  121.5 0.6 copy.90
  122.1 2.1 %multiply_reduce_fusion = (f32[768]{0:T(1024)}, f32[128]{0:T(128)S(1)}, f32[128,768]{1,0:T(8,128)S(1)}) fusion(f32[128,768]{1,0:T(8,128)S(1)} %get-tuple-element.27, f32[128]{0:T(128)} %copy-done.56, f32[768]{0:T(1024)} %copy-done.27, bf16[128,8]{0,1:T(8,128)(2,1)S(1)} %select_reduce_fusion, bf16[8,768]{1,0:T(8,128)(2,1)S(1)} %slice.118, ...), kind=kOutput, calls=%fused_computation.85 | convolution fusion | flops 2358400 | bytes 1594368 | tf_op jit(solution)/shard_map/te,de->td/dot_general | solution.py:588
  124.3 1.1 convert_add_fusion
  125.4 1.5 convolution_convert_fusion.10
  127.5 0.8 fusion.19
  128.3 0.8 fusion.20
  129.1 1.9 convolution_convert_fusion.8
  131.0 2.4 %convolution_convert_fusion.6.refs_0_ = bf16[128,768]{1,0:T(8,128)(2,1)} fusion(bf16[768,768]{1,0:T(8,128)(2,1)} %bitcast.131, bf16[128,192]{0,1:T(8,128)(2,1)} %bitcast.147, bf16[128,192]{0,1:T(8,128)(2,1)} %bitcast.143, bf16[128,192]{0,1:T(8,128)(2,1)} %bitcast.141), kind=kOutput, calls=%fused_computation.31 | convolution fusion | flops 113786880 | bytes 1327104 | tf_op jit(solution)/shard_map/tj,dj->td/dot_general | solution.py:638
  133.4 12.8 %shard_map.199 = bf16[4,128,768]{2,1,0:T(8,128)(2,1)} custom-call(bf16[128,768]{1,0:T(8,128)(2,1)} %convolution_convert_fusion.6.refs_0_), custom_call_target="tpu_custom_call" | custom-call | tf_op jit(solution)/shard_map/pallas_call | solution.py:106
  146.2 1.3 convert_reduce_fusion
  147.5 0.7 copy-done.4
  148.2 0.8 fusion.36
  149.2 1.4 maximum_bitcast_fusion.refs_0_
  150.6 1.3 rev.8
  151.8 1.1 copy.98
  153.0 0.3 copy.100
  153.3 0.9 slice.160
  154.1 2.3 %reshape.234 = f32[3,128,255]{2,1,0:T(8,128)} reshape(f32[3,32640]{1,0:T(4,128)} %slice.160) | data formatting | bytes 783360 | tf_op jit(solution)/shard_map/reshape | solution.py:62
  156.5 1.0 reduce_sum.220
  157.5 0.8 fusion.56.refs_1_
  158.3 7.7 %shard_map.201 = (f32[8,10,96]{2,1,0:T(8,128)}, f32[8,3,32]{2,1,0:T(4,128)}) custom-call(f32[8,10,96]{2,1,0:T(8,128)} %maximum_bitcast_fusion.refs_0_, f32[3,32]{1,0:T(4,128)} %fusion.56.refs_1_), custom_call_target="tpu_custom_call" | custom-call | tf_op jit(solution)/shard_map/pallas_call | solution.py:106
  166.0 0.9 reduce_sum.221
  166.9 0.6 slice_bitcast_fusion.6
  167.5 0.5 slice_bitcast_fusion.7
  168.0 1.3 reduce_sum.222
  169.3 0.4 convolution_convert_fusion
  170.0 1.1 pad_maximum_fusion.1
  171.1 2.4 %copy.89 = bf16[768,768]{1,0:T(8,128)(2,1)} copy(bf16[768,768]{0,1:T(8,128)(2,1)} %pad_maximum_fusion.1) | data formatting | bytes 2359296 | tf_op jit(solution)/shard_map/concatenate | solution.py:642
  173.4 22.8 %shard_map.200 = bf16[4,96,768]{2,1,0:T(8,128)(2,1)} custom-call(bf16[8,96,768]{2,1,0:T(8,128)(2,1)} %bitcast.120), custom_call_target="tpu_custom_call" | custom-call | tf_op jit(solution)/shard_map/pallas_call | solution.py:106
  196.2 1.2 convert_reduce_fusion.2
  197.5 0.7 fusion.102
  198.2 0.7 pad_maximum_fusion.3
  199.0 2.2 %convolution_bitcast_fusion.1 = f32[1,768,768]{2,1,0:T(8,128)} fusion(bf16[512,768]{1,0:T(8,128)(2,1)S(1)} %copy-done.15, bf16[512,1536]{1,0:T(8,128)(2,1)S(1)} %bitcast.118), kind=kOutput, calls=%fused_computation.3 | convolution fusion | flops 603979776 | bytes 3932160 | tf_op jit(solution)/shard_map/rd,rf->df/dot_general | solution.py:592
  201.2 2.2 %convolution_bitcast_fusion = f32[1,768,768]{2,1,0:T(8,128)} fusion(bf16[512,768]{1,0:T(8,128)(2,1)S(1)} %copy-done.13, bf16[512,1536]{1,0:T(8,128)(2,1)S(1)} %bitcast.119), kind=kOutput, calls=%fused_computation.2 | convolution fusion | flops 603979776 | bytes 3932160 | tf_op jit(solution)/shard_map/rf,rd->fd/dot_general | solution.py:589
  203.4 0.9 fusion.35
  (199 shorter events, 4.8 us)
Async XLA Ops:
  0.6 78.8 %copy-start = (bf16[1,768,768]{2,1,0:T(8,128)(2,1)S(1)}, bf16[1,768,768]{2,1,0:T(8,128)(2,1)}, u32[]{:S(2)}) copy-start(bf16[1,768,768]{2,1,0:T(8,128)(2,1)} %param.19) | copy-start | bytes 3538948
  0.7 29.7 %copy-start.71 = (s32[31]{0:T(128)S(1)}, s32[31]{0:T(128)}, u32[]{:S(2)}) copy-start(s32[31]{0:T(128)} %constant.106.clone) | copy-start | bytes 376
  0.7 29.8 %copy-start.68 = (f32[32,3]{0,1:T(4,128)S(1)}, f32[32,3]{0,1:T(4,128)}, u32[]{:S(2)}) copy-start(f32[32,3]{0,1:T(4,128)} %param.18) | copy-start | bytes 1156
  28.4 2.9 %copy-start.47 = (f32[128]{0:T(128)}, f32[128]{0:T(128)S(1)}, u32[]{:S(2)}) copy-start(f32[128]{0:T(128)S(1)} %add_rsqrt_fusion.1) | copy-start | bytes 1540
  30.3 1.5 copy-start.19
  30.3 1.5 copy-start.21
  30.3 1.8 copy-start.25
  32.1 16.2 %copy-start.8 = (f32[3,128,128]{1,2,0:T(8,128)}, f32[3,128,128]{1,2,0:T(8,128)S(1)}, u32[]{:S(2)}) copy-start(f32[3,128,128]{1,2,0:T(8,128)S(1)} %fusion.18) | copy-start | bytes 589828
  32.1 17.5 %copy-start.2 = (bf16[128,768]{1,0:T(8,128)(2,1)S(1)}, bf16[128,768]{1,0:T(8,128)(2,1)}, u32[]{:S(2)}) copy-start(bf16[128,768]{1,0:T(8,128)(2,1)} %param.12) | copy-start | bytes 589828
  32.4 16.0 %copy-start.16 = (bf16[3,64,128]{2,1,0:T(8,128)(2,1)}, bf16[3,64,128]{2,1,0:T(8,128)(2,1)S(1)}, u32[]{:S(2)}) copy-start(bf16[3,64,128]{2,1,0:T(8,128)(2,1)S(1)} %convolution_convert_fusion.9) | copy-start | bytes 147460
  48.3 1.7 copy-start.31
  49.6 3.5 %copy-start.29 = (bf16[8,10,96]{2,1,0:T(8,128)(2,1)S(1)}, bf16[8,10,96]{2,1,0:T(8,128)(2,1)}, u32[]{:S(2)}) copy-start(bf16[8,10,96]{2,1,0:T(8,128)(2,1)} %get-tuple-element.14) | copy-start | bytes 46084
  49.7 4.5 %copy-start.6 = (bf16[128,768]{1,0:T(8,128)(2,1)S(1)}, bf16[128,768]{1,0:T(8,128)(2,1)}, u32[]{:S(2)}) copy-start(bf16[128,768]{1,0:T(8,128)(2,1)} %param.22) | copy-start | bytes 589828
  49.9 3.3 %copy-start.27 = (f32[768]{0:T(1024)}, f32[768]{0:T(1024)S(1)}, u32[]{:S(2)}) copy-start(f32[768]{0:T(1024)S(1)} %reshape.236) | copy-start | bytes 9220
  51.9 1.2 copy-start.57
  51.9 1.2 copy-start.59
  51.9 1.3 copy-start.35
  51.9 1.3 copy-start.37
  51.9 1.2 copy-start.39
  51.9 1.2 copy-start.41
  52.0 1.2 copy-start.43
  52.0 1.2 copy-start.45
  52.0 1.1 copy-start.61
  52.0 1.1 copy-start.63
  52.0 1.3 copy-start.65
  54.1 25.3 %copy-start.50 = (f32[128]{0:T(128)}, f32[128]{0:T(128)S(1)}, u32[]{:S(2)}) copy-start(f32[128]{0:T(128)S(1)} %get-tuple-element.45) | copy-start | bytes 1540
  79.5 2.2 %copy-start.1 = (bf16[4,8,16,1536]{3,2,1,0:T(8,128)(2,1)S(1)}, bf16[4,8,16,1536]{3,2,1,0:T(8,128)(2,1)}, u32[]{:S(2)}) copy-start(bf16[4,8,16,1536]{3,2,1,0:T(8,128)(2,1)} %shard_map.197) | copy-start | bytes 4718596
  79.5 2.2 %copy-start.67 = (bf16[1,768,768]{2,1,0:T(8,128)(2,1)S(1)}, bf16[1,768,768]{2,1,0:T(8,128)(2,1)}, u32[]{:S(2)}) copy-start(bf16[1,768,768]{2,1,0:T(8,128)(2,1)} %param.20) | copy-start | bytes 3538948
  81.6 2.0 copy-start.12
  116.2 2.7 %copy-start.7 = (bf16[4,8,16,1536]{3,2,1,0:T(8,128)(2,1)S(1)}, bf16[4,8,16,1536]{3,2,1,0:T(8,128)(2,1)}, u32[]{:S(2)}) copy-start(bf16[4,8,16,1536]{3,2,1,0:T(8,128)(2,1)} %shard_map.198) | copy-start | bytes 4718596
  116.2 2.7 %copy-start.36 = (s32[512]{0:T(512)S(1)}, s32[512]{0:T(512)}, u32[]{:S(2)}) copy-start(s32[512]{0:T(512)} %copy-done.35) | copy-start | bytes 6148
  116.3 2.7 %copy-start.38 = (s32[512]{0:T(512)S(1)}, s32[512]{0:T(512)}, u32[]{:S(2)}) copy-start(s32[512]{0:T(512)} %copy-done.37) | copy-start | bytes 6148
  116.3 2.7 %copy-start.40 = (s32[512]{0:T(512)S(1)}, s32[512]{0:T(512)}, u32[]{:S(2)}) copy-start(s32[512]{0:T(512)} %copy-done.39) | copy-start | bytes 6148
  116.3 2.7 %copy-start.42 = (s32[512]{0:T(512)S(1)}, s32[512]{0:T(512)}, u32[]{:S(2)}) copy-start(s32[512]{0:T(512)} %copy-done.41) | copy-start | bytes 6148
  116.3 2.7 %copy-start.44 = (s32[512]{0:T(512)S(1)}, s32[512]{0:T(512)}, u32[]{:S(2)}) copy-start(s32[512]{0:T(512)} %copy-done.43) | copy-start | bytes 6148
  116.3 2.7 %copy-start.46 = (s32[512]{0:T(512)S(1)}, s32[512]{0:T(512)}, u32[]{:S(2)}) copy-start(s32[512]{0:T(512)} %copy-done.45) | copy-start | bytes 6148
  116.3 2.7 %copy-start.58 = (s32[128]{0:T(128)S(1)}, s32[128]{0:T(128)}, u32[]{:S(2)}) copy-start(s32[128]{0:T(128)} %copy-done.57) | copy-start | bytes 1540
  116.3 2.7 %copy-start.62 = (pred[512]{0:T(512)(128)(4,1)S(1)}, pred[512]{0:T(512)(128)(4,1)}, u32[]{:S(2)}) copy-start(pred[512]{0:T(512)(128)(4,1)} %copy-done.61) | copy-start | bytes 1540
  116.3 2.7 %copy-start.64 = (pred[512]{0:T(512)(128)(4,1)S(1)}, pred[512]{0:T(512)(128)(4,1)}, u32[]{:S(2)}) copy-start(pred[512]{0:T(512)(128)(4,1)} %copy-done.63) | copy-start | bytes 1540
  116.3 2.7 %copy-start.66 = (pred[512]{0:T(512)(128)(4,1)S(1)}, pred[512]{0:T(512)(128)(4,1)}, u32[]{:S(2)}) copy-start(pred[512]{0:T(512)(128)(4,1)} %copy-done.65) | copy-start | bytes 1540
  119.1 2.1 %copy-start.10 = (f32[128,1536]{1,0:T(8,128)}, f32[128,1536]{1,0:T(8,128)S(1)}, u32[]{:S(2)}) copy-start(f32[128,1536]{1,0:T(8,128)S(1)} %fusion.101) | copy-start | bytes 2359300
  119.1 1.1 copy-start.51
  119.1 1.1 copy-start.53
  119.1 2.1 %copy-start.34 = (f32[128,2]{0,1:T(2,128)S(1)}, f32[128,2]{0,1:T(2,128)}, u32[]{:S(2)}) copy-start(f32[128,2]{0,1:T(2,128)} %copy-done.33) | copy-start | bytes 3076
  119.1 2.1 %copy-start.55 = (f32[128]{0:T(128)S(1)}, f32[128]{0:T(128)}, u32[]{:S(2)}) copy-start(f32[128]{0:T(128)} %copy-done.54) | copy-start | bytes 1540
  119.1 2.1 %copy-start.32 = (s32[128,2]{0,1:T(2,128)S(1)}, s32[128,2]{0,1:T(2,128)}, u32[]{:S(2)}) copy-start(s32[128,2]{0,1:T(2,128)} %param.21) | copy-start | bytes 3076
  122.1 4.8 %copy-start.17 = (bf16[3,64,128]{2,1,0:T(8,128)(2,1)S(1)}, bf16[3,64,128]{2,1,0:T(8,128)(2,1)}, u32[]{:S(2)}) copy-start(bf16[3,64,128]{2,1,0:T(8,128)(2,1)} %copy-done.16) | copy-start | bytes 147460
  122.1 4.8 %copy-start.9 = (f32[3,128,128]{1,2,0:T(8,128)S(1)}, f32[3,128,128]{1,2,0:T(8,128)}, u32[]{:S(2)}) copy-start(f32[3,128,128]{1,2,0:T(8,128)} %copy-done.8) | copy-start | bytes 589828
  124.2 2.9 %copy-start.26 = (bf16[128,192]{0,1:T(8,128)(2,1)S(1)}, bf16[128,192]{0,1:T(8,128)(2,1)}, u32[]{:S(2)}) copy-start(bf16[128,192]{0,1:T(8,128)(2,1)} %copy-done.25) | copy-start | bytes 147460
  124.2 3.2 %copy-start.22 = (bf16[128,192]{0,1:T(8,128)(2,1)S(1)}, bf16[128,192]{0,1:T(8,128)(2,1)}, u32[]{:S(2)}) copy-start(bf16[128,192]{0,1:T(8,128)(2,1)} %copy-done.21) | copy-start | bytes 147460
  124.3 4.0 %copy-start.20 = (bf16[128,192]{0,1:T(8,128)(2,1)S(1)}, bf16[128,192]{0,1:T(8,128)(2,1)}, u32[]{:S(2)}) copy-start(bf16[128,192]{0,1:T(8,128)(2,1)} %copy-done.19) | copy-start | bytes 147460
  130.9 17.3 %copy-start.3 = (bf16[128,768]{1,0:T(8,128)(2,1)S(1)}, bf16[128,768]{1,0:T(8,128)(2,1)}, u32[]{:S(2)}) copy-start(bf16[128,768]{1,0:T(8,128)(2,1)} %param.12) | copy-start | bytes 589828
  131.0 17.3 %copy-start.48 = (f32[128]{0:T(128)S(1)}, f32[128]{0:T(128)}, u32[]{:S(2)}) copy-start(f32[128]{0:T(128)} %copy-done.47) | copy-start | bytes 1540
  133.4 15.7 %copy-start.30 = (f32[768]{0:T(1024)S(1)}, f32[768]{0:T(1024)}, u32[]{:S(2)}) copy-start(f32[768]{0:T(1024)} %get-tuple-element.18) | copy-start | bytes 9220
  152.9 4.6 %copy-start.70 = (s32[128]{0:T(128)S(1)}, s32[128]{0:T(128)}, u32[]{:S(2)}) copy-start(s32[128]{0:T(128)} %copy-done.69) | copy-start | bytes 1540
  152.9 16.3 %copy-start.23 = (bf16[3,64,128]{2,1,0:T(8,128)(2,1)S(1)}, bf16[3,64,128]{2,1,0:T(8,128)(2,1)}, u32[]{:S(2)}) copy-start(bf16[3,64,128]{2,1,0:T(8,128)(2,1)} %fusion.19) | copy-start | bytes 147460
  153.0 16.3 %copy-start.24 = (bf16[3,64,128]{2,1,0:T(8,128)(2,1)S(1)}, bf16[3,64,128]{2,1,0:T(8,128)(2,1)}, u32[]{:S(2)}) copy-start(bf16[3,64,128]{2,1,0:T(8,128)(2,1)} %fusion.20) | copy-start | bytes 147460
  153.0 16.3 %copy-start.28 = (bf16[3,64,128]{2,1,0:T(8,128)(2,1)S(1)}, bf16[3,64,128]{2,1,0:T(8,128)(2,1)}, u32[]{:S(2)}) copy-start(bf16[3,64,128]{2,1,0:T(8,128)(2,1)} %convolution_convert_fusion.8) | copy-start | bytes 147460
  153.0 16.3 %copy-start.49 = (f32[128]{0:T(128)S(1)}, f32[128]{0:T(128)}, u32[]{:S(2)}) copy-start(f32[128]{0:T(128)} %copy-done.47) | copy-start | bytes 1540
  154.1 15.6 %copy-start.18 = (bf16[3,64,128]{2,1,0:T(8,128)(2,1)S(1)}, bf16[3,64,128]{2,1,0:T(8,128)(2,1)}, u32[]{:S(2)}) copy-start(bf16[3,64,128]{2,1,0:T(8,128)(2,1)} %copy-done.16) | copy-start | bytes 147460
  196.2 2.7 %copy-start.15 = (bf16[512,768]{1,0:T(8,128)(2,1)S(1)}, bf16[512,768]{1,0:T(8,128)(2,1)}, u32[]{:S(2)}) copy-start(bf16[512,768]{1,0:T(8,128)(2,1)} %copy-done.14) | copy-start | bytes 2359300
  199.0 2.2 %copy-start.13 = (bf16[512,768]{1,0:T(8,128)(2,1)S(1)}, bf16[512,768]{1,0:T(8,128)(2,1)}, u32[]{:S(2)}) copy-start(bf16[512,768]{1,0:T(8,128)(2,1)} %copy-done.12) | copy-start | bytes 2359300
  201.2 2.2 %copy-start.60 = (f32[128]{0:T(128)S(1)}, f32[128]{0:T(128)}, u32[]{:S(2)}) copy-start(f32[128]{0:T(128)} %get-tuple-element.21) | copy-start | bytes 1540
  201.2 2.2 %copy-start.5 = (f32[128,768]{1,0:T(8,128)S(1)}, f32[128,768]{1,0:T(8,128)}, u32[]{:S(2)}) copy-start(f32[128,768]{1,0:T(8,128)} %copy-done.4) | copy-start | bytes 1179652
  (8 other events, 6.3 us)
